TPU v7x, 32 devices: a whole 2x2x4 slice. The times are simulated.
32 devices in a mesh: blocks: 8 (over y, x, core), slab: 4 (over z).
Axes of the slice: x: 2, y: 2, z: 4, core: 2. Of those that a mesh axis runs over, the one named last changes fastest.
Arguments:
- populations: float32 [19, 4, 8, 4096], P(None, 'slab', 'blocks'), may hold values from -6 to 6
- w_in: bfloat16 [512, 19], replicated, may hold values from -1.25 to 1.25
- w_mid: bfloat16 [1, 512, 512], replicated, may hold values from -0.25 to 0.25
- w_out: bfloat16 [19, 512], replicated, may hold values from -0.25 to 0.25
- cotangent: float32 [19, 4, 8, 4096], P(None, 'slab', 'blocks'), may hold values from -6 to 6
- face_source: int32 [8, 4], replicated, may hold values from 0 to 7, as said below
- face_level: int32 [4, 8, 6], P('slab', 'blocks'), may hold values 0 or 1
- face_quadrant: int32 [4, 8, 6], P('slab', 'blocks'), may hold values from 0 to 3
Outputs:
- final: float32 [19, 4, 8, 4096], P(None, 'slab', 'blocks')
- grad_pops: float32 [19, 4, 8, 4096], P(None, 'slab', 'blocks')
- grad_in: float32 [512, 19], replicated
- grad_mid: float32 [1, 512, 512], replicated
- grad_out: float32 [19, 512], replicated
Inputs may be any that keep to these rules, and one draw needn't show every extreme that they name: face_source is symmetric: face_source[face_source[b, f], f xor 1] = b. The +y and -y neighbours of block b are the same block, b xor 1. Every neighbour's index differs from the block's by at most 3 modulo 8, never by 0, and that distance is reached.
All inputs are finite; a program needn't handle non-finite values. No bound on the sum of `face_level` on one device may be relied on, other than what follows from the above.
Results may differ from a plain program's by a relative error of at most 0.0088.
Values sent between devices are 32-bit elements; how exact they have to be, the bound alone decides.
A program may use at most 128 MiB of HBM per device.

v0:
```python
from functools import partial

import jax
import jax.numpy as jnp
from jax import lax
from jax.sharding import PartitionSpec as P

Q = 19
HID = 512
MIDS = 1
S = 16
STEPS = 2
REACH = 3
CELLS = 4096


VELOCITIES = [
    (0, 0, 0),
    (1, 0, 0),
    (-1, 0, 0),
    (0, 1, 0),
    (0, -1, 0),
    (0, 0, 1),
    (0, 0, -1),
    (1, 1, 0),
    (-1, -1, 0),
    (1, -1, 0),
    (-1, 1, 0),
    (1, 0, 1),
    (-1, 0, -1),
    (1, 0, -1),
    (-1, 0, 1),
    (0, 1, 1),
    (0, -1, -1),
    (0, 1, -1),
    (0, -1, 1),
]
OPPOSITE = [0, 2, 1, 4, 3, 6, 5, 8, 7, 10, 9, 12, 11, 14, 13, 16, 15, 18, 17]


def from_behind(value, axis, steps):
    count = lax.axis_size(axis)
    pairs = [(source, (source + steps) % count) for source in range(count)]
    return lax.ppermute(value, axis, pairs)


def partner(x, axis, distance):
    return lax.ppermute(x, axis, [(i, i ^ 1 << distance) for i in range(lax.axis_size(axis))])


def padded(block, sides, width):
    for axis, dim in sides:
        count = lax.axis_size(axis)
        forward = [(i, i + 1) for i in range(count - 1)]
        forward.append((count - 1, 0))
        backward = [(target, source) for source, target in forward]
        low = lax.ppermute(
            lax.slice_in_dim(block, block.shape[dim] - width, None, axis=dim), axis, forward
        )
        high = lax.ppermute(lax.slice_in_dim(block, 0, width, axis=dim), axis, backward)
        block = jnp.concatenate([low, block, high], axis=dim)
    return block


def face_members(face_id):
    along = face_id // 2
    sign_value = 1 if face_id % 2 == 0 else -1
    return [which for which in range(19) if VELOCITIES[which][along] == sign_value]


def face_layers(collided, block_side):
    cube_view = collided.reshape(collided.shape[0], block_side, block_side, block_side)
    sheets = []
    for face_id in range(6):
        along = face_id // 2
        layer_index = block_side - 1 if face_id % 2 == 0 else 0
        members = jnp.stack([cube_view[which] for which in face_members(face_id)])
        layer_sheet = lax.index_in_dim(members, layer_index, along + 1, keepdims=False)
        sheets.append(layer_sheet.reshape(5, block_side * block_side))
    return jnp.stack(sheets)


def refine_all(sheets, levels, quadrant, block_side):
    area = block_side * block_side
    half_side = block_side // 2
    target = lax.iota(jnp.int32, area)
    row_part = target // block_side
    col_part = target % block_side
    src_row = quadrant[:, None] // 2 * half_side + row_part[None, :] // 2
    src_col = quadrant[:, None] % 2 * half_side + col_part[None, :] // 2
    source = jnp.where(levels[:, None] == 1, src_row * block_side + src_col, target[None, :])
    picker = (lax.iota(jnp.int32, area)[None, :, None] == source[:, None, :]).astype(jnp.float32)
    return jnp.einsum("fps,fst->fpt", sheets, picker, precision=lax.Precision.HIGHEST)


def spread_sheet(square, along, block_side):
    if along == 0:
        return jnp.tile(square, block_side)
    if along == 2:
        return jnp.repeat(square, block_side)
    plane = square.reshape(block_side, 1, block_side)
    return jnp.broadcast_to(plane, (block_side, block_side, block_side)).reshape(-1)


def stream_block(collided, ghosts, block_side):
    area = block_side * block_side
    flat_ids = lax.iota(jnp.int32, area * block_side)
    coords = [flat_ids // area, flat_ids // block_side % block_side, flat_ids % block_side]
    results = []
    for which in range(19):
        vector = VELOCITIES[which]
        offset = vector[0] * area + vector[1] * block_side + vector[2]
        shifted = jnp.roll(collided[which], offset)
        crossed = jnp.zeros(flat_ids.shape, jnp.int32)
        ghost_sum = jnp.zeros(flat_ids.shape, jnp.float32)
        for along in range(3):
            if vector[along] != 0:
                leaving = coords[along] == (0 if vector[along] == 1 else block_side - 1)
                face_id = 2 * along + (0 if vector[along] == -1 else 1)
                position = face_members(face_id ^ 1).index(which)
                others = [other for other in range(3) if other != along]
                square = jnp.roll(
                    ghosts[face_id, position], vector[others[0]] * block_side + vector[others[1]]
                )
                volume = spread_sheet(square, along, block_side)
                ghost_sum = ghost_sum + jnp.where(leaving, volume, jnp.float32(0.0))
                crossed = crossed + leaving.astype(jnp.int32)
        chosen = jnp.where(
            crossed == 0, shifted, jnp.where(crossed == 1, ghost_sum, collided[OPPOSITE[which]])
        )
        results.append(chosen)
    return jnp.stack(results)


def contract(left, right):
    return lax.dot_general(
        left, right, (((1,), (1,)), ((), ())), preferred_element_type=jnp.float32
    )


def squared(hidden):
    wide_value = hidden.astype(jnp.float32)
    return wide_value * wide_value


def collide_forward(state, w_in, w_mid, w_out):
    inputs_bf = state.astype(jnp.bfloat16)
    layers = [
        jnp.tanh(jnp.dot(w_in, inputs_bf, preferred_element_type=jnp.float32)).astype(jnp.bfloat16)
    ]
    layers.append(
        jnp.tanh(jnp.dot(w_mid[0], layers[-1], preferred_element_type=jnp.float32)).astype(
            jnp.bfloat16
        )
    )
    collided = state + jnp.dot(w_out, layers[-1], preferred_element_type=jnp.float32)
    return (collided, inputs_bf, layers)


def collide_backward(collided_bar, inputs_bf, layers, w_in, w_mid, w_out):
    delta_bf = collided_bar.astype(jnp.bfloat16)
    grad_out = contract(delta_bf, layers[-1])
    signal = (
        jnp.dot(w_out.T, delta_bf, preferred_element_type=jnp.float32) * (1.0 - squared(layers[-1]))
    ).astype(jnp.bfloat16)
    mid_parts = []
    for depth in reversed(range(w_mid.shape[0])):
        mid_parts.insert(0, contract(signal, layers[depth]))
        signal = (
            jnp.dot(w_mid[depth].T, signal, preferred_element_type=jnp.float32)
            * (1.0 - squared(layers[depth]))
        ).astype(jnp.bfloat16)
    grad_in = contract(signal, inputs_bf)
    state_bar = collided_bar + jnp.dot(w_in.T, signal, preferred_element_type=jnp.float32)
    return (state_bar, grad_in, jnp.stack(mid_parts), grad_out)


def select_pieces(pieces, slot_ids, flipped):
    total = jnp.zeros(pieces[0].shape, jnp.float32)
    for index_value in range(len(pieces)):
        chosen = jnp.stack([pieces[index_value][face_pick] for face_pick in flipped])
        total = total + jnp.where(
            (slot_ids == index_value)[:, None, None], chosen, jnp.float32(0.0)
        )
    return total


def shards(populations, w_in, w_mid, w_out, cotangent, face_source, face_level, face_quadrant):
    state = populations[:, 0, 0, :]
    levels = face_level[0, 0]
    quadrant = face_quadrant[0, 0]
    position = lax.axis_index("blocks")
    block_total = lax.axis_size("blocks")
    neighbours = lax.dynamic_index_in_dim(face_source, position, 0, keepdims=False)
    distance = (neighbours - position + block_total) % block_total
    distance = jnp.where(distance > block_total // 2, distance - block_total, distance)
    slot_ids = distance + REACH
    offsets = [step for step in range(-REACH, REACH + 1)]

    def advance(collided, lateral, from_below, from_above):
        sheets = jnp.concatenate([lateral, from_above[None], from_below[None]], axis=0)
        ghosts = refine_all(sheets, levels, quadrant, S)
        return stream_block(collided, ghosts, S)

    history = []
    for step_id in range(STEPS):
        collided, inputs_bf, layers = collide_forward(state, w_in, w_mid, w_out)
        outward, layer_pull = jax.vjp(partial(face_layers, block_side=S), collided)
        fetch_outward = outward[:4]
        x_faces = fetch_outward[:2]
        fetch_pieces = []
        for fetch_step in offsets:
            if fetch_step == 0:
                fetch_pieces.append(x_faces)
            else:
                fetch_pieces.append(from_behind(x_faces, "blocks", -fetch_step))
        x_ghosts = select_pieces(fetch_pieces, slot_ids[:2], [1, 0])
        y_ghosts = partner(fetch_outward[2:], "blocks", 0)
        lateral = jnp.concatenate([x_ghosts, y_ghosts[::-1]], axis=0)
        vertical = padded(jnp.stack([outward[5], outward[4]]), (("slab", 0),), 1)
        state, stream_pull = jax.vjp(advance, collided, lateral, vertical[0], vertical[3])
        history.append((inputs_bf, layers, layer_pull, stream_pull))
    state_bar = cotangent[:, 0, 0, :]
    totals = (
        jnp.zeros((HID, Q), jnp.float32),
        jnp.zeros((MIDS, HID, HID), jnp.float32),
        jnp.zeros((Q, HID), jnp.float32),
    )
    for step_id in reversed(range(STEPS)):
        inputs_bf, layers, layer_pull, stream_pull = history[step_id]
        local_bar, lateral_bar, below_bar, above_bar = stream_pull(state_bar)
        x_bar = lateral_bar[:2]
        pieces = []
        for return_step in offsets:
            if return_step == 0:
                pieces.append(x_bar)
            else:
                pieces.append(from_behind(x_bar, "blocks", -return_step))
        x_back = select_pieces(pieces, slot_ids[:2], [1, 0])
        y_back = partner(lateral_bar[2:], "blocks", 0)
        outward_lateral_bar = jnp.concatenate([x_back, y_back[::-1]], axis=0)
        vertical_bar = padded(jnp.stack([below_bar, above_bar]), (("slab", 0),), 1)
        outward_bar = jnp.concatenate(
            [outward_lateral_bar, vertical_bar[3][None], vertical_bar[0][None]], axis=0
        )
        (pulled_bar,) = layer_pull(outward_bar)
        collided_bar = local_bar + pulled_bar
        state_bar, part_in, part_mid, part_out = collide_backward(
            collided_bar, inputs_bf, layers, w_in, w_mid, w_out
        )
        step_grads = (part_in, part_mid, part_out)
        totals = (totals[0] + step_grads[0], totals[1] + step_grads[1], totals[2] + step_grads[2])
    totals = lax.psum((totals[0], totals[1], totals[2]), ("blocks", "slab"))
    cell_total = block_total * lax.axis_size("slab") * CELLS
    grad_scale = float(cell_total) ** (-0.5)
    return (
        state[:, None, None, :],
        state_bar[:, None, None, :],
        totals[0] * grad_scale,
        totals[1] * grad_scale,
        totals[2] * grad_scale,
    )


def solution(mesh):
    in_specs = (
        P(None, "slab", "blocks", None),
        P(),
        P(),
        P(),
        P(None, "slab", "blocks", None),
        P(),
        P("slab", "blocks", None),
        P("slab", "blocks", None),
    )
    out_specs = (P(None, "slab", "blocks", None), P(None, "slab", "blocks", None), P(), P(), P())
    return jax.shard_map(shards, mesh=mesh, in_specs=in_specs, out_specs=out_specs, check_vma=False)
```

profile of v0, /device:TPU:0, one launch (start us, length us, event | category | flops | bytes accessed | tf_op | source)
XLA Modules:
  0.0 656.2 jit_solution(16440128109553951080)
XLA Ops:
  7.3 1.7 slice_reduce_fusion.75
  36.5 2.4 collective-permute-start.26
  38.9 1.5 collective-permute-start.25
  42.4 1.8 collective-permute-start.18
  56.2 2.9 tanh_convert_fusion.2
  83.9 1.5 slice.1806
  85.4 1.7 copy.50
  87.0 1.5 slice.1803
  88.5 1.7 copy.44
  90.2 1.5 slice.1796
  91.6 1.5 slice.1789
  93.1 1.5 slice.1755
  96.2 1.4 squeeze.64
  101.6 1.6 constant_dynamic-update-slice_fusion.26
  107.4 1.9 pad_add_fusion.24
  134.3 2.3 collective-permute-start.19
  139.6 3.3 collective-permute-start.4
  144.9 1.7 collective-permute-start.1
  149.6 2.9 collective-permute-start.7
  153.8 11.7 %collective-permute-start.21 = (f32[2,5,256]{2,1,0:T(8,128)}, f32[2,5,256]{2,1,0:T(8,128)S(1)}, u32[]{:S(2)}, u32[]{:S(2)}) collective-permute-start(f32[2,5,256]{2,1,0:T(8,128)} %get-tuple-element.307), channel_id=1, source_target_pairs={{0,12},{4,16},{8,20},{12,24},{16,28},{20,0},{24,4},{28,8},{1,13},{... | collective-permute-start | bytes 30728 | tf_op jit(solution)/shard_map/ppermute | solution.py:44
  176.0 2.2 pad_add_fusion.1
  178.3 2.1 copy.88
  180.6 3.8 reshape.3258
  206.3 2.4 tanh_convert_fusion
  210.6 2.2 fusion.63
  212.8 4.8 multiply_convert_fusion.2
  234.1 1.8 collective-permute-start.13
  237.2 6.8 %fusion.395 = f32[512,512]{1,0:T(8,128)} fusion(bf16[4096,512]{1,0:T(8,128)(2,1)} %multiply_convert_fusion.2, bf16[4096,512]{1,0:T(8,128)(2,1)} %copy-done.1), kind=kOutput, calls=%fused_computation.1207 | convolution fusion | flops 2147483648 | bytes 9437184 | tf_op jit(solution)/shard_map/dot_general | solution.py:136
  244.4 2.8 multiply_convert_fusion.1
  247.5 2.0 fusion.3
  310.3 4.3 collective-permute-start.28
  320.7 2.4 collective-permute-start.34
  324.5 4.1 collective-permute-start.16
  330.0 4.1 collective-permute-done.17
  344.5 1.6 collective-permute-start.29
  353.0 2.2 pad_add_fusion
  355.3 2.1 copy.93
  357.7 3.8 reshape.3259
  362.0 4.9 multiply_convert_fusion
  366.9 3.0 convolution_add_fusion.1
  369.9 4.8 fusion
  375.0 3.3 fusion.10
  383.9 4.1 convolution_add_fusion.2
  395.5 1.5 maximum_select_fusion.44
  401.4 3.9 fusion.5
  407.9 101.2 %all-reduce.379.cloned.1.call-done = (f32[512,19]{0,1:T(8,128)}, f32[19,512]{1,0:T(8,128)}) async-done(((f32[512,19]{0,1:T(8,128)}, f32[19,512]{1,0:T(8,128)}), (f32[512,19]{0,1:T(8,128)}, f32[19,512]{1,0:T(8,128)})) %all-reduce.379.cloned.1.call-update) | async-done | bytes 77840 | tf_op jit(solution)/shard_map/psum | solution.py:253
  511.9 134.6 %all-reduce.377.cloned.1.call-done = f32[1,512,512]{2,1,0:T(8,128)} async-done(((f32[1,512,512]{2,1,0:T(8,128)}), f32[1,512,512]{2,1,0:T(8,128)}) %all-reduce.377.cloned.1.call-update) | async-done | bytes 1048592 | tf_op jit(solution)/shard_map/psum | solution.py:253
  646.5 2.3 broadcast_multiply_fusion
  (1669 shorter events, 266.7 us)
Async XLA Ops:
  7.2 49.0 %copy-start = (bf16[1,512,512]{2,1,0:T(8,128)(2,1)S(1)}, bf16[1,512,512]{2,1,0:T(8,128)(2,1)}, u32[]{:S(2)}) copy-start(bf16[1,512,512]{2,1,0:T(8,128)(2,1)} %param.10) | copy-start | bytes 1572868
  7.2 501.9 %all-reduce.379.cloned.1.call-start = ((), (), s32[]{:S(2)}) async-start(), calls=%async_computation.1 | async-start | bytes 196608 | tf_op jit(solution)/shard_map/psum | solution.py:253
  36.5 103.1 %collective-permute-start.26 = (f32[2,5,256]{2,1,0:T(8,128)}, f32[2,5,256]{2,1,0:T(8,128)}, u32[]{:S(2)}, u32[]{:S(2)}) collective-permute-start(f32[2,5,256]{2,1,0:T(8,128)} %get-tuple-element.307), channel_id=1, source_target_pairs={{0,20},{4,24},{8,28},{12,0},{16,4},{20,8},{24,12},{28,16},{1,21},{... | collective-permute-start | bytes 30728 | tf_op jit(solution)/shard_map/ppermute | solution.py:44
  38.9 104.8 %collective-permute-start.25 = (f32[2,5,256]{2,1,0:T(8,128)}, f32[2,5,256]{2,1,0:T(8,128)}, u32[]{:S(2)}, u32[]{:S(2)}) collective-permute-start(f32[2,5,256]{2,1,0:T(8,128)} %get-tuple-element.307), channel_id=1, source_target_pairs={{0,24},{4,28},{8,0},{12,4},{16,8},{20,12},{24,16},{28,20},{1,25},{... | collective-permute-start | bytes 30728 | tf_op jit(solution)/shard_map/ppermute | solution.py:44
  40.4 127.7 %collective-permute-start.24 = (f32[2,5,256]{2,1,0:T(8,128)}, f32[2,5,256]{2,1,0:T(8,128)}, u32[]{:S(2)}, u32[]{:S(2)}) collective-permute-start(f32[2,5,256]{2,1,0:T(8,128)} %get-tuple-element.307), channel_id=1, source_target_pairs={{0,28},{4,0},{8,4},{12,8},{16,12},{20,16},{24,20},{28,24},{1,29},{... | collective-permute-start | bytes 30728 | tf_op jit(solution)/shard_map/ppermute | solution.py:44
  41.8 127.7 %collective-permute-start.23 = (f32[2,5,256]{2,1,0:T(8,128)}, f32[2,5,256]{2,1,0:T(8,128)}, u32[]{:S(2)}, u32[]{:S(2)}) collective-permute-start(f32[2,5,256]{2,1,0:T(8,128)} %get-tuple-element.307), channel_id=1, source_target_pairs={{0,4},{4,8},{8,12},{12,16},{16,20},{20,24},{24,28},{28,0},{1,5},{5... | collective-permute-start | bytes 30728 | tf_op jit(solution)/shard_map/ppermute | solution.py:44
  42.4 91.8 %collective-permute-start.18 = (f32[1,5,256]{2,1,0:T(8,128)}, f32[1,5,256]{2,1,0:T(8,128)}, u32[]{:S(2)}, u32[]{:S(2)}) collective-permute-start(f32[1,5,256]{2,1,0:T(8,128)} %get-tuple-element.302), channel_id=1, source_target_pairs={{0,1},{1,2},{2,3},{3,0},{4,5},{5,6},{6,7},{7,4},{8,9},{9,10},{10,1... | collective-permute-start | bytes 15368 | tf_op jit(solution)/shard_map/ppermute | solution.py:57
  103.9 48.5 %copy-start.43 = (f32[1,5,256]{2,1,0:T(8,128)S(1)}, f32[1,5,256]{2,1,0:T(8,128)}, u32[]{:S(2)}) copy-start(f32[1,5,256]{2,1,0:T(8,128)} %squeeze.64) | copy-start | bytes 15364
  103.9 48.5 %copy-start.263 = (pred[2]{0:T(512)(128)(4,1)S(1)}, pred[2]{0:T(512)(128)(4,1)}, u32[]{:S(2)}) copy-start(pred[2]{0:T(512)(128)(4,1)} %get-tuple-element.512) | copy-start | bytes 10
  103.9 48.5 %copy-start.265 = (pred[2]{0:T(512)(128)(4,1)S(1)}, pred[2]{0:T(512)(128)(4,1)}, u32[]{:S(2)}) copy-start(pred[2]{0:T(512)(128)(4,1)} %get-tuple-element.513) | copy-start | bytes 10
  104.0 48.5 %copy-start.267 = (pred[2]{0:T(512)(128)(4,1)S(1)}, pred[2]{0:T(512)(128)(4,1)}, u32[]{:S(2)}) copy-start(pred[2]{0:T(512)(128)(4,1)} %get-tuple-element.514) | copy-start | bytes 10
  104.1 61.4 %copy-start.260 = (f32[2,5,256]{2,1,0:T(8,128)S(1)}, f32[2,5,256]{2,1,0:T(8,128)}, u32[]{:S(2)}) copy-start(f32[2,5,256]{2,1,0:T(8,128)} %get-tuple-element.306) | copy-start | bytes 30724
  104.1 62.7 %copy-start.278 = (s32[6,256]{1,0:T(8,128)S(1)}, s32[6,256]{1,0:T(8,128)}, u32[]{:S(2)}) copy-start(s32[6,256]{1,0:T(8,128)} %copy-done.277) | copy-start | bytes 18436
  134.3 4.0 collective-permute-start.19
  138.3 6.1 collective-permute-start.5
  139.6 5.3 collective-permute-start.4
  143.7 3.0 collective-permute-start.3
  144.4 4.1 collective-permute-start.2
  144.9 4.6 collective-permute-start.1
  146.6 5.8 collective-permute-start
  148.5 4.2 collective-permute-start.6
  149.6 4.3 collective-permute-start.7
  152.4 13.0 %collective-permute-start.8 = (f32[1,5,256]{2,1,0:T(8,128)S(1)}, f32[1,5,256]{2,1,0:T(8,128)S(1)}, u32[]{:S(2)}, u32[]{:S(2)}) collective-permute-start(f32[1,5,256]{2,1,0:T(8,128)S(1)} %squeeze.59), channel_id=1, source_target_pairs={{0,1},{1,2},{2,3},{3,0},{4,5},{5,6},{6,7},{7,4},{8,9},{9,10},{10,1... | collective-permute-start | bytes 15368 | tf_op jit(solution)/shard_map/ppermute | solution.py:57
  152.7 18.2 %collective-permute-start.22 = (f32[2,5,256]{2,1,0:T(8,128)}, f32[2,5,256]{2,1,0:T(8,128)S(1)}, u32[]{:S(2)}, u32[]{:S(2)}) collective-permute-start(f32[2,5,256]{2,1,0:T(8,128)} %get-tuple-element.307), channel_id=1, source_target_pairs={{0,8},{4,12},{8,16},{12,20},{16,24},{20,28},{24,0},{28,4},{1,9},{5... | collective-permute-start | bytes 30728 | tf_op jit(solution)/shard_map/ppermute | solution.py:44
  153.8 17.7 %collective-permute-start.21 = (f32[2,5,256]{2,1,0:T(8,128)}, f32[2,5,256]{2,1,0:T(8,128)S(1)}, u32[]{:S(2)}, u32[]{:S(2)}) collective-permute-start(f32[2,5,256]{2,1,0:T(8,128)} %get-tuple-element.307), channel_id=1, source_target_pairs={{0,12},{4,16},{8,20},{12,24},{16,28},{20,0},{24,4},{28,8},{1,13},{... | collective-permute-start | bytes 30728 | tf_op jit(solution)/shard_map/ppermute | solution.py:44
  165.5 7.0 %collective-permute-start.20 = (f32[2,5,256]{2,1,0:T(8,128)S(1)}, f32[2,5,256]{2,1,0:T(8,128)S(1)}, u32[]{:S(2)}, u32[]{:S(2)}) collective-permute-start(f32[2,5,256]{2,1,0:T(8,128)S(1)} %copy-done.260), channel_id=1, source_target_pairs={{0,4},{4,0},{8,12},{12,8},{16,20},{20,16},{24,28},{28,24},{1,5},{5... | collective-permute-start | bytes 30728 | tf_op jit(solution)/shard_map/ppermute | solution.py:48
  233.7 83.5 %collective-permute-start.14 = (f32[2,5,256]{2,1,0:T(8,128)}, f32[2,5,256]{2,1,0:T(8,128)}, u32[]{:S(2)}, u32[]{:S(2)}) collective-permute-start(f32[2,5,256]{2,1,0:T(8,128)} %constant_dynamic-update-slice_fusion.42), channel_id=1, source_target_pairs={{0,20},{4,24},{8,28},{12,0},{16,4},{20,8},{24,12},{28,16},{1,21},{... | collective-permute-start | bytes 30728 | tf_op jit(solution)/shard_map/ppermute | solution.py:44
  234.1 85.0 %collective-permute-start.13 = (f32[2,5,256]{2,1,0:T(8,128)}, f32[2,5,256]{2,1,0:T(8,128)}, u32[]{:S(2)}, u32[]{:S(2)}) collective-permute-start(f32[2,5,256]{2,1,0:T(8,128)} %constant_dynamic-update-slice_fusion.42), channel_id=1, source_target_pairs={{0,24},{4,28},{8,0},{12,4},{16,8},{20,12},{24,16},{28,20},{1,25},{... | collective-permute-start | bytes 30728 | tf_op jit(solution)/shard_map/ppermute | solution.py:44
  235.9 84.8 %collective-permute-start.12 = (f32[2,5,256]{2,1,0:T(8,128)}, f32[2,5,256]{2,1,0:T(8,128)}, u32[]{:S(2)}, u32[]{:S(2)}) collective-permute-start(f32[2,5,256]{2,1,0:T(8,128)} %constant_dynamic-update-slice_fusion.42), channel_id=1, source_target_pairs={{0,28},{4,0},{8,4},{12,8},{16,12},{20,16},{24,20},{28,24},{1,29},{... | collective-permute-start | bytes 30728 | tf_op jit(solution)/shard_map/ppermute | solution.py:44
  237.2 86.6 %collective-permute-start.11 = (f32[2,5,256]{2,1,0:T(8,128)}, f32[2,5,256]{2,1,0:T(8,128)}, u32[]{:S(2)}, u32[]{:S(2)}) collective-permute-start(f32[2,5,256]{2,1,0:T(8,128)} %constant_dynamic-update-slice_fusion.42), channel_id=1, source_target_pairs={{0,4},{4,8},{8,12},{12,16},{16,20},{20,24},{24,28},{28,0},{1,5},{5... | collective-permute-start | bytes 30728 | tf_op jit(solution)/shard_map/ppermute | solution.py:44
  295.7 14.5 %collective-permute-start.27 = (f32[1,5,256]{2,1,0:T(8,128)S(1)}, f32[1,5,256]{2,1,0:T(8,128)S(1)}, u32[]{:S(2)}, u32[]{:S(2)}) collective-permute-start(f32[1,5,256]{2,1,0:T(8,128)S(1)} %copy-done.283), channel_id=1, source_target_pairs={{0,1},{1,2},{2,3},{3,0},{4,5},{5,6},{6,7},{7,4},{8,9},{9,10},{10,1... | collective-permute-start | bytes 15368 | tf_op jit(solution)/shard_map/ppermute | solution.py:57
  295.8 48.7 %copy-start.261 = (f32[2,5,256]{2,1,0:T(8,128)S(1)}, f32[2,5,256]{2,1,0:T(8,128)}, u32[]{:S(2)}) copy-start(f32[2,5,256]{2,1,0:T(8,128)} %get-tuple-element.300) | copy-start | bytes 30724
  295.8 52.8 %copy-start.129 = (f32[1,5,256]{2,1,0:T(8,128)S(1)}, f32[1,5,256]{2,1,0:T(8,128)}, u32[]{:S(2)}) copy-start(f32[1,5,256]{2,1,0:T(8,128)} %get-tuple-element.297) | copy-start | bytes 15364
  295.8 52.8 %copy-start.130 = (f32[1,5,256]{2,1,0:T(8,128)S(1)}, f32[1,5,256]{2,1,0:T(8,128)}, u32[]{:S(2)}) copy-start(f32[1,5,256]{2,1,0:T(8,128)} %get-tuple-element.298) | copy-start | bytes 15364
  310.3 5.7 collective-permute-start.28
  315.9 8.6 %collective-permute-start.10 = (f32[2,5,256]{2,1,0:T(8,128)}, f32[2,5,256]{2,1,0:T(8,128)S(1)}, u32[]{:S(2)}, u32[]{:S(2)}) collective-permute-start(f32[2,5,256]{2,1,0:T(8,128)} %constant_dynamic-update-slice_fusion.42), channel_id=1, source_target_pairs={{0,8},{4,12},{8,16},{12,20},{16,24},{20,28},{24,0},{28,4},{1,9},{5... | collective-permute-start | bytes 30728 | tf_op jit(solution)/shard_map/ppermute | solution.py:44
  317.1 11.5 %collective-permute-start.9 = (f32[2,5,256]{2,1,0:T(8,128)}, f32[2,5,256]{2,1,0:T(8,128)S(1)}, u32[]{:S(2)}, u32[]{:S(2)}) collective-permute-start(f32[2,5,256]{2,1,0:T(8,128)} %constant_dynamic-update-slice_fusion.42), channel_id=1, source_target_pairs={{0,12},{4,16},{8,20},{12,24},{16,28},{20,0},{24,4},{28,8},{1,13},{... | collective-permute-start | bytes 30728 | tf_op jit(solution)/shard_map/ppermute | solution.py:44
  319.1 24.8 %collective-permute-start.35 = (f32[2,5,256]{2,1,0:T(8,128)S(1)}, f32[2,5,256]{2,1,0:T(8,128)S(1)}, u32[]{:S(2)}, u32[]{:S(2)}) collective-permute-start(f32[2,5,256]{2,1,0:T(8,128)S(1)} %copy-done.262), channel_id=1, source_target_pairs={{0,20},{4,24},{8,28},{12,0},{16,4},{20,8},{24,12},{28,16},{1,21},{... | collective-permute-start | bytes 30728 | tf_op jit(solution)/shard_map/ppermute | solution.py:44
  320.7 23.8 %collective-permute-start.34 = (f32[2,5,256]{2,1,0:T(8,128)S(1)}, f32[2,5,256]{2,1,0:T(8,128)S(1)}, u32[]{:S(2)}, u32[]{:S(2)}) collective-permute-start(f32[2,5,256]{2,1,0:T(8,128)S(1)} %copy-done.262), channel_id=1, source_target_pairs={{0,24},{4,28},{8,0},{12,4},{16,8},{20,12},{24,16},{28,20},{1,25},{... | collective-permute-start | bytes 30728 | tf_op jit(solution)/shard_map/ppermute | solution.py:44
  323.8 5.0 collective-permute-start.15
  324.5 5.5 collective-permute-start.16
  328.6 5.4 collective-permute-start.17
  328.8 17.4 %collective-permute-start.33 = (f32[2,5,256]{2,1,0:T(8,128)S(1)}, f32[2,5,256]{2,1,0:T(8,128)S(1)}, u32[]{:S(2)}, u32[]{:S(2)}) collective-permute-start(f32[2,5,256]{2,1,0:T(8,128)S(1)} %copy-done.262), channel_id=1, source_target_pairs={{0,28},{4,0},{8,4},{12,8},{16,12},{20,16},{24,20},{28,24},{1,29},{... | collective-permute-start | bytes 30728 | tf_op jit(solution)/shard_map/ppermute | solution.py:44
  330.0 16.9 %collective-permute-start.32 = (f32[2,5,256]{2,1,0:T(8,128)S(1)}, f32[2,5,256]{2,1,0:T(8,128)S(1)}, u32[]{:S(2)}, u32[]{:S(2)}) collective-permute-start(f32[2,5,256]{2,1,0:T(8,128)S(1)} %copy-done.262), channel_id=1, source_target_pairs={{0,4},{4,8},{8,12},{12,16},{16,20},{20,24},{24,28},{28,0},{1,5},{5... | collective-permute-start | bytes 30728 | tf_op jit(solution)/shard_map/ppermute | solution.py:44
  334.1 13.9 %collective-permute-start.31 = (f32[2,5,256]{2,1,0:T(8,128)S(1)}, f32[2,5,256]{2,1,0:T(8,128)S(1)}, u32[]{:S(2)}, u32[]{:S(2)}) collective-permute-start(f32[2,5,256]{2,1,0:T(8,128)S(1)} %copy-done.262), channel_id=1, source_target_pairs={{0,8},{4,12},{8,16},{12,20},{16,24},{20,28},{24,0},{28,4},{1,9},{5... | collective-permute-start | bytes 30728 | tf_op jit(solution)/shard_map/ppermute | solution.py:44
  343.9 4.7 collective-permute-start.30
  344.5 5.0 collective-permute-start.29
  388.0 258.5 %all-reduce.377.cloned.1.call-start = ((), (), s32[]{:S(2)}) async-start(), calls=%async_computation | async-start | bytes 2097152 | tf_op jit(solution)/shard_map/psum | solution.py:253
  (367 other events, 3147.9 us)
Sparse Core Ops, SparseCore 0:
  388.1 120.9 all-reduce.378
  514.9 131.6 all-reduce.376
where the time goes:
time: 666 us; the launch traced here: 656 us
  waiting for transfers between devices  244 us (37%)
  local copies, waits for them, and re-layouts  170 us (26%)
  other arithmetic  111 us (17%)
  matrix products  57.1 us (9%)
  starting transfers between devices  52.2 us (8%)
  between operations  22.5 us (3%)
    psum x2, waiting for transfers between devices, shards(): totals = lax.psum((totals[0], totals[1], totals[2]), ('blocks', 'slab'))  236 us
    add_any x36, other arithmetic, stream_block(): shifted = jnp.roll(collided[which], offset)  36.3 us
    ppermute x24, starting transfers between devices, from_behind(): return lax.ppermute(value, axis, pairs)  33.5 us
    slice x36, local copies, waits for them, and re-layouts, stream_block(): shifted = jnp.roll(collided[which], offset)  23.9 us
    unnamed x824, local copies, waits for them, and re-layouts  23.9 us
    split x65, local copies, waits for them, and re-layouts, stream_block(): shifted = jnp.roll(collided[which], offset)  22.5 us
    concatenate x48, other arithmetic, stream_block(): jnp.roll(ghosts[face_id, position], vector[others[0]] * block_side + vect...  21 us
    dot_general x6, matrix products, contract(): lax.dot_general(left, right, (((1,), (1,)), ((), ())), preferred_element_...  20.7 us
  transfers between devices with their start and end apart: 38, of which 8 were waited for; matrix products, arithmetic and copies ran while one was open for 32% of the time, Pallas kernels for 0%

commit v1 on v0

v1 whole, which is shorter than its diff:
```python
import functools

import jax
import jax.numpy as jnp
import numpy as np
from jax import lax
from jax.experimental import pallas as pl
from jax.experimental.pallas import tpu as pltpu
from jax.sharding import PartitionSpec as P

REACH = 3
R = 24
S = 16
A = S * S
CHUNK = 512
MESH = pl.DeviceIdType.MESH
F32, BF16 = jnp.float32, jnp.bfloat16

VELOCITIES = [
    (0, 0, 0),
    (1, 0, 0),
    (-1, 0, 0),
    (0, 1, 0),
    (0, -1, 0),
    (0, 0, 1),
    (0, 0, -1),
    (1, 1, 0),
    (-1, -1, 0),
    (1, -1, 0),
    (-1, 1, 0),
    (1, 0, 1),
    (-1, 0, -1),
    (1, 0, -1),
    (-1, 0, 1),
    (0, 1, 1),
    (0, -1, -1),
    (0, 1, -1),
    (0, -1, 1),
]
Q = len(VELOCITIES)


def row_table():
    table = np.zeros((4, R, A), np.int32)
    for q, v in enumerate(VELOCITIES):
        for axis in range(3):
            table[axis, q] = v[axis]
        if q:
            table[3, q] = 1 if q % 2 else -1
    return table


def lane_roll(x, shift):
    shift %= A
    return x if shift == 0 else pltpu.roll(x, shift, 1)


class Geometry:
    def __init__(self, table_ref):
        lane = lax.broadcasted_iota(jnp.int32, (R, A), 1)
        y, z = lane // S, lane % S
        self.v = [table_ref[axis] for axis in range(3)]
        self.plus = [v == 1 for v in self.v]
        self.minus = [v == -1 for v in self.v]
        parity = table_ref[3]
        self.odd, self.even = parity == 1, parity == -1
        py, my, pz, mz = self.plus[1], self.minus[1], self.plus[2], self.minus[2]
        self.ly = (py & (y == 0)) | (my & (y == S - 1))
        self.lz = (pz & (z == 0)) | (mz & (z == S - 1))
        self.oy = (py & (y == S - 1)) | (my & (y == 0))
        self.oz = (pz & (z == S - 1)) | (mz & (z == 0))

    def row_roll(self, x, axis, step, sign=1):
        up, down = lane_roll(x, sign * step), lane_roll(x, -sign * step)
        return jnp.where(self.plus[axis], up, jnp.where(self.minus[axis], down, x))

    def opposite(self, x):
        return jnp.where(self.odd, pltpu.roll(x, R - 1, 0), jnp.where(self.even, pltpu.roll(x, 1, 0), x))

    def leaving_x(self, k):
        if k == 0:
            return self.plus[0]
        if k == S - 1:
            return self.minus[0]
        return None

    def crossings(self, k):
        ly, lz, lx = self.ly, self.lz, self.leaving_x(k)
        two, some = ly & lz, ly | lz
        if lx is None:
            return ly & ~lz, lz & ~ly, None, two, ~some
        return (
            ly & ~lz & ~lx,
            lz & ~ly & ~lx,
            lx & ~some,
            two | (lx & some),
            ~(some | lx),
        )


def layer(ref, k):
    return ref[:, k * A : (k + 1) * A]


def put(ref, k, value):
    ref[:, k * A : (k + 1) * A] = value


def split3(x):
    hi = x.astype(BF16)
    rest = x - hi.astype(F32)
    mid = rest.astype(BF16)
    low = (rest - mid.astype(F32)).astype(BF16)
    return jnp.concatenate([hi, mid, low], axis=0)


def refine(g, sheet, axis, pick_ref, transposed):
    parts = split3(sheet)
    dims = (((1,), (1 if transposed else 0,)), ((), ()))
    both = []
    for face in (2 * axis, 2 * axis + 1):
        r = lax.dot_general(parts, pick_ref[face], dims, preferred_element_type=F32)
        both.append(r[:R] + r[R : 2 * R] + r[2 * R :])
    return jnp.where(g.minus[axis], both[0], both[1])


def gather_sheets(g, ref, sheets_ref):
    acc_y = acc_z = None
    for k in range(S):
        a = layer(ref, k)
        ty = lane_roll(jnp.where(g.oy, a, 0.0), S * k)
        tz = lane_roll(jnp.where(g.oz, a, 0.0), k)
        acc_y = ty if acc_y is None else acc_y + ty
        acc_z = tz if acc_z is None else acc_z + tz
    sheet_x = jnp.where(g.plus[0], layer(ref, S - 1), jnp.where(g.minus[0], layer(ref, 0), 0.0))
    sheets_ref[0, :R] = sheet_x
    sheets_ref[1, :R] = jnp.where(g.plus[1], lane_roll(acc_y, S), acc_y)
    sheets_ref[2, :R] = jnp.where(g.plus[2], lane_roll(acc_z, -(S - 1)), acc_z)


def gather_bars(g, ref, pick_ref, sheets_ref):
    acc_x = acc_y = acc_z = None
    for k in range(S):
        b = layer(ref, k)
        one_y, one_z, one_x, _, _ = g.crossings(k)
        ty = lane_roll(jnp.where(one_y, b, 0.0), S * k)
        tz = lane_roll(jnp.where(one_z, b, 0.0), k)
        acc_y = ty if acc_y is None else acc_y + ty
        acc_z = tz if acc_z is None else acc_z + tz
        if one_x is not None:
            tx = jnp.where(one_x, b, 0.0)
            acc_x = tx if acc_x is None else acc_x + tx
    acc_y = jnp.where(g.minus[1], lane_roll(acc_y, S), acc_y)
    acc_z = jnp.where(g.minus[2], lane_roll(acc_z, -(S - 1)), acc_z)
    gx = g.row_roll(g.row_roll(acc_x, 1, S, -1), 2, 1, -1)
    gy = g.row_roll(g.row_roll(acc_y, 0, S, -1), 2, 1, -1)
    gz = g.row_roll(g.row_roll(acc_z, 1, S, -1), 0, 1, -1)
    for axis, value in enumerate((gx, gy, gz)):
        sheets_ref[axis, R:] = refine(g, value, axis, pick_ref, True)


def stream(g, post_ref, recv_ref, slot_ref, pick_ref, out_ref, rows):
    from_plus, from_minus = recv_ref[slot_ref[0], :R], recv_ref[slot_ref[1], :R]
    raw_x = jnp.where(g.minus[0], from_plus, from_minus)
    raw_y = recv_ref[2 * REACH, :R]
    raw_z = jnp.where(g.minus[2], recv_ref[2 * REACH + 1, :R], recv_ref[2 * REACH + 2, :R])
    gx, gy, gz = (refine(g, raw, axis, pick_ref, False) for axis, raw in enumerate((raw_x, raw_y, raw_z)))
    sx = g.row_roll(g.row_roll(gx, 1, S), 2, 1)
    sy = g.row_roll(g.row_roll(gy, 0, S), 2, 1)
    sz = g.row_roll(g.row_roll(gz, 1, S), 0, 1)
    sy = jnp.where(g.minus[1], lane_roll(sy, -S), sy)
    sz = jnp.where(g.minus[2], lane_roll(sz, S - 1), sz)
    for k in range(S):
        here = layer(post_ref, k)
        behind = layer(post_ref, max(k - 1, 0))
        ahead = layer(post_ref, min(k + 1, S - 1))
        moved = jnp.where(g.plus[0], behind, jnp.where(g.minus[0], ahead, here))
        moved = g.row_roll(g.row_roll(moved, 1, S), 2, 1)
        one_y, one_z, one_x, two, _ = g.crossings(k)
        out = jnp.where(one_y, lane_roll(sy, -S * k), moved)
        out = jnp.where(one_z, lane_roll(sz, -k), out)
        if one_x is not None:
            out = jnp.where(one_x, sx, out)
        out = jnp.where(two, g.opposite(here), out)
        out_ref[:, k * A : (k + 1) * A] = out[:rows]


def stream_back(g, bar_ref, recv_ref, slot_ref, work_ref, out_ref):
    from_plus, from_minus = recv_ref[slot_ref[0], R:], recv_ref[slot_ref[1], R:]
    ox = jnp.where(g.plus[0], from_plus, from_minus)
    oy = recv_ref[2 * REACH, R:]
    oz = jnp.where(g.plus[2], recv_ref[2 * REACH + 1, R:], recv_ref[2 * REACH + 2, R:])
    oy = jnp.where(g.plus[1], lane_roll(oy, -S), oy)
    oz = jnp.where(g.plus[2], lane_roll(oz, S - 1), oz)
    for k in range(S):
        put(work_ref, k, jnp.where(g.crossings(k)[4], layer(bar_ref, k), 0.0))
    for k in range(S):
        zero = jnp.zeros((R, A), F32)
        ahead = layer(work_ref, k + 1) if k + 1 < S else zero
        behind = layer(work_ref, k - 1) if k > 0 else zero
        moved = jnp.where(g.plus[0], ahead, jnp.where(g.minus[0], behind, layer(work_ref, k)))
        out = g.row_roll(g.row_roll(moved, 1, S, -1), 2, 1, -1)
        out += g.opposite(jnp.where(g.crossings(k)[3], layer(bar_ref, k), 0.0))
        out += jnp.where(g.oy, lane_roll(oy, -S * k), 0.0)
        out += jnp.where(g.oz, lane_roll(oz, -k), 0.0)
        if k == 0:
            out += jnp.where(g.minus[0], ox, 0.0)
        if k == S - 1:
            out += jnp.where(g.plus[0], ox, 0.0)
        put(out_ref, k, out)


def mm(a, b):
    return jnp.dot(a, b, preferred_element_type=F32)


def outer(a, b):
    return lax.dot_general(a, b, (((1,), (1,)), ((), ())), preferred_element_type=F32)


def slope(h):
    wide = h.astype(F32)
    return 1.0 - wide * wide


def collide(x, w_in, w_mid, w_out):
    inputs = x.astype(BF16)
    h0 = jnp.tanh(mm(w_in[...], inputs)).astype(BF16)
    h1 = jnp.tanh(mm(w_mid[...], h0)).astype(BF16)
    return inputs, h0, h1, x + mm(w_out[...], h1)


def collide_back(bar, inputs, h0, h1, w_in_t, w_mid_t, w_out_t, grads_ref, hid):
    e = bar.astype(BF16)
    a1 = (mm(w_out_t[...], e) * slope(h1)).astype(BF16)
    a0 = (mm(w_mid_t[...], a1) * slope(h0)).astype(BF16)
    grads_ref[:hid] += outer(a1, h0)
    grads_ref[hid : hid + R] += outer(inputs, a0)
    grads_ref[hid + R : hid + 2 * R] += outer(e, h1)
    return bar + mm(w_in_t[...], a0)


def span(i):
    return pl.ds(pl.multiple_of(i * CHUNK, CHUNK), CHUNK)


def load_rows(dst, src):
    dst[...] = jnp.zeros(dst.shape, F32)
    dst[:Q] = src[...]


def first_kernel(
    table, pick, pops, cot, w_in, w_mid, w_out, post, h_hbm, sheets, wide, cot_wide, h_buf, sems
):
    g = Geometry(table)
    cells = pops.shape[1]
    load_rows(wide, pops)
    load_rows(cot_wide, cot)

    def moved(i, j):
        return pltpu.make_async_copy(h_buf.at[j, :, span(i)], h_hbm.at[j, :, span(i)], sems.at[j, i])

    @pl.loop(0, cells // CHUNK)
    def _(i):
        at = span(i)
        _, h0, h1, out = collide(wide[:, at], w_in, w_mid, w_out)
        post[:, at] = out
        h_buf[0, :, at] = h0
        h_buf[1, :, at] = h1
        moved(i, 0).start()
        moved(i, 1).start()

    gather_sheets(g, post, sheets)
    gather_bars(g, cot_wide, pick, sheets)

    @pl.loop(0, cells // CHUNK)
    def _(i):
        moved(i, 0).wait()
        moved(i, 1).wait()


def middle_kernel(
    slots, table, pick, recv, post1, cot, w_in, w_mid, w_out, w_in_t, w_mid_t, w_out_t,
    post2, bar, sheets, grads, state, wide, work, pbar,
):
    g = Geometry(table)
    cells = post1.shape[1]
    hid = w_mid.shape[0]
    load_rows(wide, cot)
    stream(g, post1, recv, slots, pick, state, R)
    stream_back(g, wide, recv, slots, work, pbar)
    grads[...] = jnp.zeros(grads.shape, F32)

    @pl.loop(0, cells // CHUNK)
    def _(i):
        at = span(i)
        inputs, h0, h1, out = collide(state[:, at], w_in, w_mid, w_out)
        post2[:, at] = out
        bar[:, at] = collide_back(pbar[:, at], inputs, h0, h1, w_in_t, w_mid_t, w_out_t, grads, hid)

    gather_sheets(g, post2, sheets)
    gather_bars(g, bar, pick, sheets)


def last_kernel(
    slots, table, pick, recv, post2, bar, pops, h_hbm, grads_in, w_in_t, w_mid_t, w_out_t,
    final, grad_pops, grads, wide, work, pbar, h_buf, sems,
):
    g = Geometry(table)
    cells = post2.shape[1]
    hid = w_mid_t.shape[0]

    def moved(i, j):
        return pltpu.make_async_copy(h_hbm.at[j, :, span(i)], h_buf.at[j, :, span(i)], sems.at[j, i])

    @pl.loop(0, cells // CHUNK)
    def _(i):
        moved(i, 0).start()
        moved(i, 1).start()

    load_rows(wide, pops)
    stream(g, post2, recv, slots, pick, final, Q)
    stream_back(g, bar, recv, slots, work, pbar)
    grads[...] = grads_in[...]

    @pl.loop(0, cells // CHUNK)
    def _(i):
        at = span(i)
        moved(i, 0).wait()
        moved(i, 1).wait()
        out = collide_back(
            pbar[:, at], wide[:, at].astype(BF16), h_buf[0, :, at], h_buf[1, :, at],
            w_in_t, w_mid_t, w_out_t, grads, hid,
        )
        grad_pops[:, at] = out[:Q]


OFFSETS = [d for d in range(-REACH, REACH + 1) if d != 0]


def exchange_kernel(blocks, slabs, sheets, recv, send_sem, recv_sem):
    me, level = lax.axis_index("blocks"), lax.axis_index("slab")
    side = [lax.rem(me - d + blocks, blocks) for d in OFFSETS]
    other = me + 1 - 2 * lax.rem(me, 2)
    above, below = lax.rem(level + 1, slabs), lax.rem(level + slabs - 1, slabs)
    barrier = pltpu.get_barrier_semaphore()
    for target in side:
        pl.semaphore_signal(barrier, inc=1, device_id={"blocks": target}, device_id_type=MESH)
    for target in (above, below):
        pl.semaphore_signal(barrier, inc=1, device_id={"slab": target}, device_id_type=MESH)
    pl.semaphore_wait(barrier, len(side) + 2)
    plan = [(0, i, {"blocks": target}) for i, target in enumerate(side)]
    plan.append((1, len(side), {"blocks": other}))
    plan.append((2, len(side) + 1, {"slab": below}))
    plan.append((2, len(side) + 2, {"slab": above}))
    copies = []
    for which, slot, device in plan:
        copy = pltpu.make_async_remote_copy(
            src_ref=sheets.at[which], dst_ref=recv.at[slot],
            send_sem=send_sem.at[slot], recv_sem=recv_sem.at[slot],
            device_id=device, device_id_type=MESH,
        )
        copy.start()
        copies.append(copy)
    for copy in copies:
        copy.wait()


def sum_kernel(blocks, slabs, grads, out, land_b, land_s, part, sems_b, sems_s, gath_b, gath_s):
    me, level = lax.axis_index("blocks"), lax.axis_index("slab")
    rows, width = grads.shape[0] // blocks, grads.shape[1] // slabs
    barrier = pltpu.get_barrier_semaphore()
    peer_b = [lax.rem(me + d, blocks) for d in range(1, blocks)]
    peer_s = [lax.rem(level + d, slabs) for d in range(1, slabs)]
    for t in peer_b:
        pl.semaphore_signal(barrier, inc=1, device_id={"blocks": t}, device_id_type=MESH)
    for t in peer_s:
        pl.semaphore_signal(barrier, inc=1, device_id={"slab": t}, device_id_type=MESH)
    pl.semaphore_wait(barrier, blocks + slabs - 2)

    def row_of(i):
        return pl.ds(pl.multiple_of(i * rows, 8), rows)

    def lane_of(i):
        return pl.ds(pl.multiple_of(i * width, 128), width)

    def send(src, dst, sems, i, axis, target):
        copy = pltpu.make_async_remote_copy(
            src_ref=src, dst_ref=dst, send_sem=sems.at[0, i], recv_sem=sems.at[1, i],
            device_id={axis: target}, device_id_type=MESH,
        )
        copy.start()
        return copy

    copies = [send(grads.at[row_of(t)], land_b.at[i], sems_b, i, "blocks", t) for i, t in enumerate(peer_b)]
    total = grads[row_of(me)]
    for i, copy in enumerate(copies):
        copy.wait()
        total += land_b[i]
    part[...] = total
    copies = [send(part.at[:, lane_of(t)], land_s.at[i], sems_s, i, "slab", t) for i, t in enumerate(peer_s)]
    mine = part[:, lane_of(level)]
    for i, copy in enumerate(copies):
        copy.wait()
        mine += land_s[i]
    out[row_of(me), lane_of(level)] = mine
    spot = out.at[row_of(me), lane_of(level)]
    copies = [send(spot, spot, gath_s, i, "slab", t) for i, t in enumerate(peer_s)]
    for copy in copies:
        copy.wait()
    spot = out.at[row_of(me)]
    copies = [send(spot, spot, gath_b, i, "blocks", t) for i, t in enumerate(peer_b)]
    for copy in copies:
        copy.wait()


def pickers(levels, quadrant):
    swapped = quadrant % 2 * 2 + quadrant // 2
    quadrant = jnp.where(jnp.arange(6) >= 4, swapped, quadrant)
    target = lax.iota(jnp.int32, A)
    row, col = target // S, target % S
    half = S // 2
    src = (quadrant[:, None] // 2 * half + row // 2) * S + quadrant[:, None] % 2 * half + col // 2
    source = jnp.where(levels[:, None] == 1, src, target[None, :])
    return (target[None, :, None] == source[:, None, :]).astype(BF16)


def vmem(count):
    return [pl.BlockSpec(memory_space=pltpu.VMEM)] * count


SMEM_SPEC = pl.BlockSpec(memory_space=pltpu.SMEM)
ANY_SPEC = pl.BlockSpec(memory_space=pl.ANY)
LIMIT = 60 * 1024 * 1024


def shape(dims, dtype=F32):
    return jax.ShapeDtypeStruct(dims, dtype)


def shards(blocks, slabs, populations, w_in, w_mid, w_out, cotangent, face_source, face_level, face_quadrant):
    cells = populations.shape[-1]
    hid = w_in.shape[0]
    pops, cot = populations[:, 0, 0, :], cotangent[:, 0, 0, :]
    table = jnp.asarray(row_table())
    pick = pickers(face_level[0, 0], face_quadrant[0, 0])
    position = lax.axis_index("blocks")
    neighbours = lax.dynamic_index_in_dim(face_source, position, 0, keepdims=False)
    distance = (neighbours - position + blocks) % blocks
    distance = jnp.where(distance > blocks // 2, distance - blocks, distance)
    slots = jnp.where(distance < 0, distance + REACH, distance + REACH - 1)[:2]
    slots = jnp.clip(slots, 0, 2 * REACH - 1)
    w_in = jnp.pad(w_in, ((0, 0), (0, R - Q)))
    w_out = jnp.pad(w_out, ((0, R - Q), (0, 0)))
    w_mid = w_mid[0]
    backs = (w_in.T, w_mid.T, w_out.T)
    step = 8 * blocks
    total_rows = -(-(hid + 2 * R) // step) * step
    parts = cells // CHUNK
    volume = pltpu.VMEM((R, cells), F32)
    params = pltpu.CompilerParams(vmem_limit_bytes=LIMIT)

    def exchange(sheets, which):
        count = 2 * REACH + 3
        return pl.pallas_call(
            functools.partial(exchange_kernel, blocks, slabs),
            out_shape=shape((count, 2 * R, A)),
            in_specs=vmem(1),
            out_specs=vmem(1)[0],
            scratch_shapes=[pltpu.SemaphoreType.DMA((count,)), pltpu.SemaphoreType.DMA((count,))],
            compiler_params=pltpu.CompilerParams(collective_id=which, has_side_effects=True),
            name=f"exchange{which}",
        )(sheets)

    post1, hidden, sheets = pl.pallas_call(
        first_kernel,
        out_shape=(shape((R, cells)), shape((2, hid, cells), BF16), shape((3, 2 * R, A))),
        in_specs=vmem(7),
        out_specs=(vmem(1)[0], ANY_SPEC, vmem(1)[0]),
        scratch_shapes=[volume, volume, pltpu.VMEM((2, hid, cells), BF16), pltpu.SemaphoreType.DMA((2, parts))],
        compiler_params=params,
        name="first",
    )(table, pick, pops, cot, w_in, w_mid, w_out)
    recv = exchange(sheets, 0)
    post2, bar, sheets, grads = pl.pallas_call(
        middle_kernel,
        out_shape=(shape((R, cells)), shape((R, cells)), shape((3, 2 * R, A)), shape((total_rows, hid))),
        in_specs=[SMEM_SPEC] + vmem(11),
        out_specs=tuple(vmem(4)),
        scratch_shapes=[volume] * 4,
        compiler_params=params,
        name="middle",
    )(slots, table, pick, recv, post1, cot, w_in, w_mid, w_out, *backs)
    recv = exchange(sheets, 1)
    final, grad_pops, grads = pl.pallas_call(
        last_kernel,
        out_shape=(shape((Q, cells)), shape((Q, cells)), shape((total_rows, hid))),
        in_specs=[SMEM_SPEC] + vmem(6) + [ANY_SPEC] + vmem(4),
        out_specs=tuple(vmem(3)),
        scratch_shapes=[volume] * 3 + [pltpu.VMEM((2, hid, cells), BF16), pltpu.SemaphoreType.DMA((2, parts))],
        compiler_params=params,
        name="last",
    )(slots, table, pick, recv, post2, bar, pops, hidden, grads, *backs)
    rows, width = total_rows // blocks, hid // slabs
    total = pl.pallas_call(
        functools.partial(sum_kernel, blocks, slabs),
        out_shape=shape((total_rows, hid)),
        in_specs=vmem(1),
        out_specs=vmem(1)[0],
        scratch_shapes=[
            pltpu.VMEM((blocks - 1, rows, hid), F32),
            pltpu.VMEM((slabs - 1, rows, width), F32),
            pltpu.VMEM((rows, hid), F32),
            pltpu.SemaphoreType.DMA((2, blocks - 1)),
            pltpu.SemaphoreType.DMA((2, slabs - 1)),
            pltpu.SemaphoreType.DMA((2, blocks - 1)),
            pltpu.SemaphoreType.DMA((2, slabs - 1)),
        ],
        compiler_params=pltpu.CompilerParams(collective_id=2, has_side_effects=True),
        name="sum_all",
    )(grads)
    total = total * float(blocks * slabs * cells) ** (-0.5)
    return (
        final[:, None, None, :],
        grad_pops[:, None, None, :],
        total[hid : hid + Q].T,
        total[:hid][None],
        total[hid + R : hid + R + Q],
    )


def solution(mesh):
    spread = P(None, "slab", "blocks", None)
    in_specs = (spread, P(), P(), P(), spread, P(), P("slab", "blocks", None), P("slab", "blocks", None))
    out_specs = (spread, spread, P(), P(), P())
    body = functools.partial(shards, mesh.shape["blocks"], mesh.shape["slab"])
    return jax.shard_map(body, mesh=mesh, in_specs=in_specs, out_specs=out_specs, check_vma=False)
```

time: 666 us -> 133 us (0.20); the launches traced: 656 us -> 132 us
  waiting for transfers between devices: 244 us -> 0 us
  local copies, waits for them, and re-layouts: 170 us -> 13.3 us
  Pallas kernels: 0 us -> 113 us
  other arithmetic: 111 us -> 5.49 us
  matrix products: 57.1 us -> 0 us
  starting transfers between devices: 52.2 us -> 0 us
  between operations: 22.5 us -> 0.71 us
    psum x2 -> x0, waiting for transfers between devices: 236 us -> none  [shards(): totals = lax.psum((totals[0], totals[1], totals[2]), ('blocks', 'slab'))]
    pallas_call x0 -> x6, Pallas kernels: none -> 113 us  [the longest x1 40.8 us: shards(): pl.pallas_call(functools.partial(sum_kernel, blocks, slabs), out_shape=sh...]
    slice x142 -> x1, local copies, waits for them, and re-layouts: 60.4 us -> 0.64 us  [shards(): total[hid + R:hid + R + Q]]
    add_any x86 -> x0, other arithmetic: 59.3 us -> none  [the longest x36 36.3 us: stream_block(): shifted = jnp.roll(collided[which], offset)]
    dot_general x22 -> x0, matrix products: 57.1 us -> none  [the longest x6 20.7 us: contract(): lax.dot_general(left, right, (((1,), (1,)), ((), ())), preferred_element_...]
    ppermute x36 -> x0, starting transfers between devices: 51.9 us -> none  [the longest x24 33.5 us: from_behind(): return lax.ppermute(value, axis, pairs)]
    split x147 -> x0, local copies, waits for them, and re-layouts: 40.2 us -> none  [the longest x65 22.5 us: stream_block(): shifted = jnp.roll(collided[which], offset)]
    concatenate x48 -> x0, other arithmetic: 21 us -> none  [stream_block(): jnp.roll(ghosts[face_id, position], vector[others[0]] * block_side + vect...]
  transfers between devices with their start and end apart: 38 -> 0, of which waited for: 8 -> 0; matrix products, arithmetic and copies ran while one was open for 32% -> 0% of each run, Pallas kernels for 0% -> 0%
where the time goes in v1:
time: 133 us; the launch traced here: 132 us
  Pallas kernels  113 us (85%)
  local copies, waits for them, and re-layouts  13.3 us (10%)
  other arithmetic  5.49 us (4%)
    pallas_call x1, Pallas kernels, shards(): pl.pallas_call(functools.partial(sum_kernel, blocks, slabs), out_shape=sh...  40.8 us
    pallas_call x2, Pallas kernels, exchange(): pl.pallas_call(functools.partial(exchange_kernel, blocks, slabs), out_sha...  23.1 us
    pallas_call x1, Pallas kernels, shards(): pl.pallas_call(middle_kernel, out_shape=(shape((R, cells)), shape((R, cel...  22.1 us
    pallas_call x1, Pallas kernels, shards(): pl.pallas_call(last_kernel, out_shape=(shape((Q, cells)), shape((Q, cells...  17 us
    pallas_call x1, Pallas kernels, shards(): pl.pallas_call(first_kernel, out_shape=(shape((R, cells)), shape((2, hid,...  9.65 us
    unnamed x13, local copies, waits for them, and re-layouts  8.22 us

profile of v1, /device:TPU:0, one launch (start us, length us, event | category | flops | bytes accessed | tf_op | source)
XLA Modules:
  0.0 132.1 jit_solution(4673036941972747140)
XLA Ops:
  0.6 0.0 copy-start
  0.6 0.9 add_reduce_fusion
  1.6 0.6 slice_clamp_fusion.slots
  2.2 0.7 compare_bitcast_fusion
  2.8 0.7 fusion.7
  3.5 0.1 iota_select_fusion
  3.6 1.4 %pad_bitcast_fusion.w_in_t = bf16[24,512]{1,0:T(8,128)(2,1)} fusion(bf16[512,19]{0,1:T(8,128)(2,1)} %param.10), kind=kLoop, calls=%fused_computation.48 | loop fusion | bytes 44032 | tf_op jit(solution)/shard_map/transpose | solution.py:456
  5.0 0.9 copy.15
  5.9 0.1 copy.30
  6.0 0.7 pad_bitcast_fusion.1.w_out_t
  6.7 0.0 copy-start.1
  6.7 0.0 copy-start.2
  6.7 0.6 pad.9.clone.w_out
  7.3 0.9 copy.29
  8.2 0.7 pad.8.clone.w_in
  8.9 0.0 copy-done
  8.9 1.0 copy.14
  9.9 1.1 fusion.pick
  11.0 0.0 copy-done.1
  11.0 0.0 copy-done.2
  11.0 1.3 copy_bitcast_fusion
  12.3 9.6 %first.1 = (f32[24,4096]{1,0:T(8,128)}, bf16[2,512,4096]{2,1,0:T(8,128)(2,1)}, f32[3,48,256]{2,1,0:T(8,128)}) custom-call(s32[4,24,256]{2,1,0:T(8,128)} %constant.133.clone.table, bf16[6,256,256]{2,1,0:T(8,128)(2,1)} %fusion.pick, f32[19,4096]{1,0:T(8,128)} %get-tuple-element.37.pops, f32[19,4096]{1,0:T(8,128)} %get-tuple-element.36.cot, ...), custom_call_target="tpu_custom_call" | custom-call | tf_op jit(solution)/shard_map/first/pallas_call | solution.py:475
  21.9 13.1 %exchange0.1.recv = f32[9,48,256]{2,1,0:T(8,128)} custom-call(f32[3,48,256]{2,1,0:T(8,128)} %get-tuple-element.15.sheets), custom_call_target="tpu_custom_call" | custom-call | tf_op jit(solution)/shard_map/exchange0/pallas_call | solution.py:465
  35.0 22.1 %middle.1 = (f32[24,4096]{1,0:T(8,128)}, f32[24,4096]{1,0:T(8,128)}, f32[3,48,256]{2,1,0:T(8,128)}, f32[576,512]{1,0:T(8,128)}) custom-call(s32[2]{0:T(128)} %slice_clamp_fusion.slots, s32[4,24,256]{2,1,0:T(8,128)} %constant.133.clone.table, bf16[6,256,256]{2,1,0:T(8,128)(2,1)} %fusion.pick, f32[9,48,256]{2,1,0:T(8,128)} %exchange0.1.recv, ...), custom_call_target="tpu_custom_call" | custom-call | tf_op jit(solution)/shard_map/middle/pallas_call | solution.py:485
  57.1 10.0 %exchange1.1.recv = f32[9,48,256]{2,1,0:T(8,128)} custom-call(f32[3,48,256]{2,1,0:T(8,128)} %get-tuple-element.17.sheets), custom_call_target="tpu_custom_call" | custom-call | tf_op jit(solution)/shard_map/exchange1/pallas_call | solution.py:465
  67.1 17.0 %last.1 = (f32[19,4096]{1,0:T(8,128)}, f32[19,4096]{1,0:T(8,128)}, f32[576,512]{1,0:T(8,128)}) custom-call(s32[2]{0:T(128)} %slice_clamp_fusion.slots, s32[4,24,256]{2,1,0:T(8,128)} %constant.133.clone.table, bf16[6,256,256]{2,1,0:T(8,128)(2,1)} %fusion.pick, f32[9,48,256]{2,1,0:T(8,128)} %exchange1.1.recv, f32[24,4096]{1,0:T(8,128)} %get-tuple-element.18.post2, ...), custom_call_target="tpu_custom_call" | custom-call | tf_op jit(solution)/shard_map/last/pallas_call | solution.py:495
  84.1 2.0 %copy.22 = f32[19,1,1,4096]{3,2,1,0:T(1,128)} copy(f32[19,1,1,4096]{3,0,2,1:T(8,128)} %bitcast.40) | data formatting | bytes 622592
  86.2 2.0 %copy.23 = f32[19,1,1,4096]{3,2,1,0:T(1,128)} copy(f32[19,1,1,4096]{3,0,2,1:T(8,128)} %bitcast.39) | data formatting | bytes 622592
  88.2 40.8 %sum_all.1 = f32[576,512]{1,0:T(8,128)} custom-call(f32[576,512]{1,0:T(8,128)} %get-tuple-element.24.grads), custom_call_target="tpu_custom_call" | custom-call | tf_op jit(solution)/shard_map/sum_all/pallas_call | solution.py:505
  129.0 1.4 %broadcast_multiply_fusion = f32[576,512]{1,0:T(8,128)S(1)} fusion(f32[576,512]{1,0:T(8,128)} %sum_all.1), kind=kLoop, calls=%fused_computation.3 | loop fusion | flops 294912 | bytes 2359296 | tf_op jit(solution)/shard_map/mul | solution.py:522
  130.4 0.6 fusion.8
  131.1 1.0 slice_bitcast_fusion
  (3 shorter events, 0.0 us)
Async XLA Ops:
  0.6 8.2 %copy-start = (bf16[1,512,512]{2,1,0:T(8,128)(2,1)S(1)}, bf16[1,512,512]{2,1,0:T(8,128)(2,1)}, u32[]{:S(2)}) copy-start(bf16[1,512,512]{2,1,0:T(8,128)(2,1)} %param.11) | copy-start | bytes 1572868
  6.7 4.3 %copy-start.1 = (f32[19,1,1,4096]{3,2,1,0:T(1,128)S(1)}, f32[19,1,1,4096]{3,2,1,0:T(1,128)}, u32[]{:S(2)}) copy-start(f32[19,1,1,4096]{3,2,1,0:T(1,128)} %param.13) | copy-start | bytes 933892
  6.7 4.3 %copy-start.2 = (f32[19,1,1,4096]{3,2,1,0:T(1,128)S(1)}, f32[19,1,1,4096]{3,2,1,0:T(1,128)}, u32[]{:S(2)}) copy-start(f32[19,1,1,4096]{3,2,1,0:T(1,128)} %param.9) | copy-start | bytes 933892

commit v2 on v1

--- a/solution.py
+++ b/solution.py
@@ -124,6 +124,34 @@
     return jnp.where(g.minus[axis], both[0], both[1])
 
 
+PACK = [
+    [(0, 1, 3), (2, 7, 15)],
+    [(0, 3, 5), (2, 7, 11), (6, 15, 19)],
+    [(0, 5, 7), (2, 11, 19)],
+]
+FACED = 10
+
+
+def pack(sheets_ref, axis, base, value):
+    for at, low, high in PACK[axis]:
+        sheets_ref[axis, base + at : base + at + high - low] = value[low:high]
+
+
+def unpack(recv_ref, slot, axis, base, tmp_ref):
+    tmp_ref[...] = jnp.zeros(tmp_ref.shape, F32)
+    for at, low, high in PACK[axis]:
+        tmp_ref[low:high] = recv_ref[slot, base + at : base + at + high - low]
+    return tmp_ref[...]
+
+
+def slot_of(source_ref, blocks, face):
+    me = lax.axis_index("blocks")
+    distance = lax.rem(source_ref[me, face] - me + blocks, blocks)
+    distance = jnp.where(distance > blocks // 2, distance - blocks, distance)
+    slot = jnp.where(distance < 0, distance + REACH, distance + REACH - 1)
+    return jnp.clip(slot, 0, 2 * REACH - 1)
+
+
 def gather_sheets(g, ref, sheets_ref):
     acc_y = acc_z = None
     for k in range(S):
@@ -133,9 +161,9 @@
         acc_y = ty if acc_y is None else acc_y + ty
         acc_z = tz if acc_z is None else acc_z + tz
     sheet_x = jnp.where(g.plus[0], layer(ref, S - 1), jnp.where(g.minus[0], layer(ref, 0), 0.0))
-    sheets_ref[0, :R] = sheet_x
-    sheets_ref[1, :R] = jnp.where(g.plus[1], lane_roll(acc_y, S), acc_y)
-    sheets_ref[2, :R] = jnp.where(g.plus[2], lane_roll(acc_z, -(S - 1)), acc_z)
+    pack(sheets_ref, 0, 0, sheet_x)
+    pack(sheets_ref, 1, 0, jnp.where(g.plus[1], lane_roll(acc_y, S), acc_y))
+    pack(sheets_ref, 2, 0, jnp.where(g.plus[2], lane_roll(acc_z, -(S - 1)), acc_z))
 
 
 def gather_bars(g, ref, pick_ref, sheets_ref):
@@ -156,14 +184,19 @@
     gy = g.row_roll(g.row_roll(acc_y, 0, S, -1), 2, 1, -1)
     gz = g.row_roll(g.row_roll(acc_z, 1, S, -1), 0, 1, -1)
     for axis, value in enumerate((gx, gy, gz)):
-        sheets_ref[axis, R:] = refine(g, value, axis, pick_ref, True)
-
-
-def stream(g, post_ref, recv_ref, slot_ref, pick_ref, out_ref, rows):
-    from_plus, from_minus = recv_ref[slot_ref[0], :R], recv_ref[slot_ref[1], :R]
-    raw_x = jnp.where(g.minus[0], from_plus, from_minus)
-    raw_y = recv_ref[2 * REACH, :R]
-    raw_z = jnp.where(g.minus[2], recv_ref[2 * REACH + 1, :R], recv_ref[2 * REACH + 2, :R])
+        pack(sheets_ref, axis, FACED, refine(g, value, axis, pick_ref, True))
+
+
+def received(g, recv_ref, slots, base, toward, tmp_ref):
+    sides = [unpack(recv_ref, slot, 0, base, tmp_ref) for slot in slots]
+    x = jnp.where(toward[0], sides[0], sides[1])
+    y = unpack(recv_ref, 2 * REACH, 1, base, tmp_ref)
+    sides = [unpack(recv_ref, 2 * REACH + side, 2, base, tmp_ref) for side in (1, 2)]
+    return x, y, jnp.where(toward[2], sides[0], sides[1])
+
+
+def stream(g, post_ref, recv_ref, slots, pick_ref, tmp_ref, store):
+    raw_x, raw_y, raw_z = received(g, recv_ref, slots, 0, g.minus, tmp_ref)
     gx, gy, gz = (refine(g, raw, axis, pick_ref, False) for axis, raw in enumerate((raw_x, raw_y, raw_z)))
     sx = g.row_roll(g.row_roll(gx, 1, S), 2, 1)
     sy = g.row_roll(g.row_roll(gy, 0, S), 2, 1)
@@ -182,14 +215,11 @@
         if one_x is not None:
             out = jnp.where(one_x, sx, out)
         out = jnp.where(two, g.opposite(here), out)
-        out_ref[:, k * A : (k + 1) * A] = out[:rows]
-
-
-def stream_back(g, bar_ref, recv_ref, slot_ref, work_ref, out_ref):
-    from_plus, from_minus = recv_ref[slot_ref[0], R:], recv_ref[slot_ref[1], R:]
-    ox = jnp.where(g.plus[0], from_plus, from_minus)
-    oy = recv_ref[2 * REACH, R:]
-    oz = jnp.where(g.plus[2], recv_ref[2 * REACH + 1, R:], recv_ref[2 * REACH + 2, R:])
+        store(k, out)
+
+
+def stream_back(g, bar_ref, recv_ref, slots, tmp_ref, work_ref, out_ref):
+    ox, oy, oz = received(g, recv_ref, slots, FACED, g.plus, tmp_ref)
     oy = jnp.where(g.plus[1], lane_roll(oy, -S), oy)
     oz = jnp.where(g.plus[2], lane_roll(oz, S - 1), oz)
     for k in range(S):
@@ -244,18 +274,57 @@
     return pl.ds(pl.multiple_of(i * CHUNK, CHUNK), CHUNK)
 
 
+LANES = 128
+
+
 def load_rows(dst, src):
-    dst[...] = jnp.zeros(dst.shape, F32)
-    dst[:Q] = src[...]
+    lines = dst.shape[1] // LANES
+    dst[16:] = jnp.zeros((R - 16, dst.shape[1]), F32)
+    for i in range(lines):
+        dst[:Q, i * LANES : (i + 1) * LANES] = src[pl.ds(i, Q, stride=lines), :]
+
+
+def store_lines(dst, first, value):
+    lines = dst.shape[0] // Q
+    for i in range(value.shape[1] // LANES):
+        dst[pl.ds(first + i, Q, stride=lines), :] = value[:Q, i * LANES : (i + 1) * LANES]
+
+
+def one_hot_layers(level, quadrant, pick):
+    half = S // 2
+    target = lax.broadcasted_iota(jnp.int32, (A, A), 1)
+    source = lax.broadcasted_iota(jnp.int32, (A, A), 0)
+    row, col = target // S, target % S
+    fine = row // 2 * S + col // 2
+    for face in range(6):
+        q = quadrant[0, 0, face]
+        high, low = q // 2, q % 2
+        if face >= 4:
+            high, low = low, high
+        corner = high * half * S + low * half
+        wanted = jnp.where(level[0, 0, face] == 1, corner + fine, target)
+        pick[face] = jnp.where(source == wanted, 1.0, 0.0).astype(BF16)
+
+
+def padded_rows(src, tall, flat, flipped):
+    tall[...] = jnp.zeros(tall.shape, F32)
+    tall[:Q] = src[...].astype(F32)
+    flat[...] = tall[...].astype(BF16)
+    flipped[...] = tall[...].T.astype(BF16)
 
 
 def first_kernel(
-    table, pick, pops, cot, w_in, w_mid, w_out, post, h_hbm, sheets, wide, cot_wide, h_buf, sems
+    level, quadrant, table, pops, cot, w_in_rows, w_mid, w_out_rows,
+    post, h_hbm, sheets, pick, w_in, w_in_t, w_out, w_out_t, wide, cot_wide, h_buf, tall, sems,
 ):
     g = Geometry(table)
-    cells = pops.shape[1]
+    cells = wide.shape[1]
     load_rows(wide, pops)
     load_rows(cot_wide, cot)
+    padded_rows(w_in_rows, tall, w_in_t, w_in)
+    padded_rows(w_out_rows, tall, w_out, w_out_t)
+    one_hot_layers(level, quadrant, pick)
+    sheets[...] = jnp.zeros(sheets.shape, F32)
 
     def moved(i, j):
         return pltpu.make_async_copy(h_buf.at[j, :, span(i)], h_hbm.at[j, :, span(i)], sems.at[j, i])
@@ -280,16 +349,18 @@
 
 
 def middle_kernel(
-    slots, table, pick, recv, post1, cot, w_in, w_mid, w_out, w_in_t, w_mid_t, w_out_t,
-    post2, bar, sheets, grads, state, wide, work, pbar,
+    blocks, source, table, pick, recv, post1, cot, w_in, w_mid, w_out, w_in_t, w_mid_t, w_out_t,
+    post2, bar, sheets, grads, state, wide, work, pbar, tmp,
 ):
     g = Geometry(table)
     cells = post1.shape[1]
     hid = w_mid.shape[0]
+    slots = [slot_of(source, blocks, face) for face in (0, 1)]
     load_rows(wide, cot)
-    stream(g, post1, recv, slots, pick, state, R)
-    stream_back(g, wide, recv, slots, work, pbar)
+    stream(g, post1, recv, slots, pick, tmp, functools.partial(put, state))
+    stream_back(g, wide, recv, slots, tmp, work, pbar)
     grads[...] = jnp.zeros(grads.shape, F32)
+    sheets[...] = jnp.zeros(sheets.shape, F32)
 
     @pl.loop(0, cells // CHUNK)
     def _(i):
@@ -303,8 +374,8 @@
 
 
 def last_kernel(
-    slots, table, pick, recv, post2, bar, pops, h_hbm, grads_in, w_in_t, w_mid_t, w_out_t,
-    final, grad_pops, grads, wide, work, pbar, h_buf, sems,
+    blocks, source, table, pick, recv, post2, bar, pops, h_hbm, grads_in, w_in_t, w_mid_t, w_out_t,
+    final, grad_pops, grads, wide, work, pbar, tmp, h_buf, sems,
 ):
     g = Geometry(table)
     cells = post2.shape[1]
@@ -318,9 +389,10 @@
         moved(i, 0).start()
         moved(i, 1).start()
 
+    slots = [slot_of(source, blocks, face) for face in (0, 1)]
     load_rows(wide, pops)
-    stream(g, post2, recv, slots, pick, final, Q)
-    stream_back(g, bar, recv, slots, work, pbar)
+    stream(g, post2, recv, slots, pick, tmp, lambda k, value: store_lines(final, k * A // LANES, value))
+    stream_back(g, bar, recv, slots, tmp, work, pbar)
     grads[...] = grads_in[...]
 
     @pl.loop(0, cells // CHUNK)
@@ -332,7 +404,9 @@
             pbar[:, at], wide[:, at].astype(BF16), h_buf[0, :, at], h_buf[1, :, at],
             w_in_t, w_mid_t, w_out_t, grads, hid,
         )
-        grad_pops[:, at] = out[:Q]
+        pbar[:, at] = out
+
+    store_lines(grad_pops, 0, pbar[...])
 
 
 OFFSETS = [d for d in range(-REACH, REACH + 1) if d != 0]
@@ -366,63 +440,82 @@
         copy.wait()
 
 
-def sum_kernel(blocks, slabs, grads, out, land_b, land_s, part, sems_b, sems_s, gath_b, gath_s):
+PIECES = 3
+
+
+def sum_kernel(chips, slabs, grads, out, land_c, half, land_t, part, land_s, sems):
     me, level = lax.axis_index("blocks"), lax.axis_index("slab")
-    rows, width = grads.shape[0] // blocks, grads.shape[1] // slabs
+    core, chip = lax.rem(me, 2), me // 2
+    rows, width = part.shape[1], land_s.shape[-1]
+    peer_t = [lax.rem(chip + d, chips) for d in range(1, chips)]
+    peer_s = [lax.rem(level + d, slabs) for d in range(1, slabs)]
+    twin = {"blocks": me + 1 - 2 * core}
+    sides = [{"blocks": 2 * t + core} for t in peer_t]
+    stack = [{"slab": t} for t in peer_s]
     barrier = pltpu.get_barrier_semaphore()
-    peer_b = [lax.rem(me + d, blocks) for d in range(1, blocks)]
-    peer_s = [lax.rem(level + d, slabs) for d in range(1, slabs)]
-    for t in peer_b:
-        pl.semaphore_signal(barrier, inc=1, device_id={"blocks": t}, device_id_type=MESH)
-    for t in peer_s:
-        pl.semaphore_signal(barrier, inc=1, device_id={"slab": t}, device_id_type=MESH)
-    pl.semaphore_wait(barrier, blocks + slabs - 2)
-
-    def row_of(i):
-        return pl.ds(pl.multiple_of(i * rows, 8), rows)
-
-    def lane_of(i):
-        return pl.ds(pl.multiple_of(i * width, 128), width)
-
-    def send(src, dst, sems, i, axis, target):
+    for device in [twin] + sides + stack:
+        pl.semaphore_signal(barrier, inc=1, device_id=device, device_id_type=MESH)
+    pl.semaphore_wait(barrier, 1 + len(sides) + len(stack))
+
+    def send(src, dst, p, which, device):
         copy = pltpu.make_async_remote_copy(
-            src_ref=src, dst_ref=dst, send_sem=sems.at[0, i], recv_sem=sems.at[1, i],
-            device_id={axis: target}, device_id_type=MESH,
+            src_ref=src, dst_ref=dst, send_sem=sems.at[0, p, which], recv_sem=sems.at[1, p, which],
+            device_id=device, device_id_type=MESH,
         )
         copy.start()
         return copy
 
-    copies = [send(grads.at[row_of(t)], land_b.at[i], sems_b, i, "blocks", t) for i, t in enumerate(peer_b)]
-    total = grads[row_of(me)]
-    for i, copy in enumerate(copies):
-        copy.wait()
-        total += land_b[i]
-    part[...] = total
-    copies = [send(part.at[:, lane_of(t)], land_s.at[i], sems_s, i, "slab", t) for i, t in enumerate(peer_s)]
-    mine = part[:, lane_of(level)]
-    for i, copy in enumerate(copies):
-        copy.wait()
-        mine += land_s[i]
-    out[row_of(me), lane_of(level)] = mine
-    spot = out.at[row_of(me), lane_of(level)]
-    copies = [send(spot, spot, gath_s, i, "slab", t) for i, t in enumerate(peer_s)]
-    for copy in copies:
-        copy.wait()
-    spot = out.at[row_of(me)]
-    copies = [send(spot, spot, gath_b, i, "blocks", t) for i, t in enumerate(peer_b)]
-    for copy in copies:
-        copy.wait()
-
-
-def pickers(levels, quadrant):
-    swapped = quadrant % 2 * 2 + quadrant // 2
-    quadrant = jnp.where(jnp.arange(6) >= 4, swapped, quadrant)
-    target = lax.iota(jnp.int32, A)
-    row, col = target // S, target % S
-    half = S // 2
-    src = (quadrant[:, None] // 2 * half + row // 2) * S + quadrant[:, None] % 2 * half + col // 2
-    source = jnp.where(levels[:, None] == 1, src, target[None, :])
-    return (target[None, :, None] == source[:, None, :]).astype(BF16)
+    def half_of(p, c):
+        return pl.ds(pl.multiple_of((2 * p + c) * chips * rows, 8), chips * rows)
+
+    def row_of(p):
+        return pl.ds(pl.multiple_of(((2 * p + core) * chips + chip) * rows, 8), rows)
+
+    def lane_of(i):
+        return pl.ds(pl.multiple_of(i * width, 128), width)
+
+    first_t, first_s = 1, len(sides) + 1
+    again = len(sides) + len(stack) + 1
+    flying = [[] for _ in range(PIECES)]
+
+    def stage(p, number):
+        for copy in flying[p]:
+            copy.wait()
+        if number == 0:
+            flying[p] = [send(grads.at[half_of(p, 1 - core)], land_c.at[p], p, 0, twin)]
+        if number == 1:
+            half[p] = grads[half_of(p, core)] + land_c[p]
+            flying[p] = [
+                send(half.at[p, pl.ds(pl.multiple_of(t * rows, 8), rows)], land_t.at[p, i], p, first_t + i, device)
+                for i, (t, device) in enumerate(zip(peer_t, sides))
+            ]
+        if number == 2:
+            total = half[p, pl.ds(pl.multiple_of(chip * rows, 8), rows)]
+            for i in range(len(sides)):
+                total += land_t[p, i]
+            part[p] = total
+            flying[p] = [
+                send(part.at[p, :, lane_of(t)], land_s.at[p, i], p, first_s + i, device)
+                for i, (t, device) in enumerate(zip(peer_s, stack))
+            ]
+        if number == 3:
+            mine = part[p, :, lane_of(level)]
+            for i in range(len(stack)):
+                mine += land_s[p, i]
+            out[row_of(p), lane_of(level)] = mine
+            spot = out.at[row_of(p), lane_of(level)]
+            flying[p] = [send(spot, spot, p, again + first_s + i, device) for i, device in enumerate(stack)]
+        if number == 4:
+            spot = out.at[row_of(p)]
+            flying[p] = [send(spot, spot, p, again + first_t + i, device) for i, device in enumerate(sides)]
+        if number == 5:
+            spot = out.at[half_of(p, core)]
+            flying[p] = [send(spot, spot, p, again, twin)]
+
+    for tick in range(6 + PIECES):
+        for p in range(PIECES):
+            if 0 <= tick - p <= 6:
+                stage(p, tick - p)
 
 
 def vmem(count):
@@ -441,30 +534,23 @@
 def shards(blocks, slabs, populations, w_in, w_mid, w_out, cotangent, face_source, face_level, face_quadrant):
     cells = populations.shape[-1]
     hid = w_in.shape[0]
-    pops, cot = populations[:, 0, 0, :], cotangent[:, 0, 0, :]
+    pops, cot = (v.reshape(Q * cells // LANES, LANES) for v in (populations, cotangent))
     table = jnp.asarray(row_table())
-    pick = pickers(face_level[0, 0], face_quadrant[0, 0])
-    position = lax.axis_index("blocks")
-    neighbours = lax.dynamic_index_in_dim(face_source, position, 0, keepdims=False)
-    distance = (neighbours - position + blocks) % blocks
-    distance = jnp.where(distance > blocks // 2, distance - blocks, distance)
-    slots = jnp.where(distance < 0, distance + REACH, distance + REACH - 1)[:2]
-    slots = jnp.clip(slots, 0, 2 * REACH - 1)
-    w_in = jnp.pad(w_in, ((0, 0), (0, R - Q)))
-    w_out = jnp.pad(w_out, ((0, R - Q), (0, 0)))
     w_mid = w_mid[0]
-    backs = (w_in.T, w_mid.T, w_out.T)
-    step = 8 * blocks
+    w_mid_t = w_mid.T
+    step = 8 * blocks * PIECES
     total_rows = -(-(hid + 2 * R) // step) * step
     parts = cells // CHUNK
     volume = pltpu.VMEM((R, cells), F32)
+    tmp = pltpu.VMEM((R, A), F32)
+    sheet_rows = 24
     params = pltpu.CompilerParams(vmem_limit_bytes=LIMIT)
 
     def exchange(sheets, which):
         count = 2 * REACH + 3
         return pl.pallas_call(
             functools.partial(exchange_kernel, blocks, slabs),
-            out_shape=shape((count, 2 * R, A)),
+            out_shape=shape((count, sheet_rows, A)),
             in_specs=vmem(1),
             out_specs=vmem(1)[0],
             scratch_shapes=[pltpu.SemaphoreType.DMA((count,)), pltpu.SemaphoreType.DMA((count,))],
@@ -472,57 +558,64 @@
             name=f"exchange{which}",
         )(sheets)
 
-    post1, hidden, sheets = pl.pallas_call(
+    post1, hidden, sheets, pick, w_in, w_in_t, w_out, w_out_t = pl.pallas_call(
         first_kernel,
-        out_shape=(shape((R, cells)), shape((2, hid, cells), BF16), shape((3, 2 * R, A))),
-        in_specs=vmem(7),
-        out_specs=(vmem(1)[0], ANY_SPEC, vmem(1)[0]),
-        scratch_shapes=[volume, volume, pltpu.VMEM((2, hid, cells), BF16), pltpu.SemaphoreType.DMA((2, parts))],
+        out_shape=(
+            shape((R, cells)), shape((2, hid, cells), BF16), shape((3, sheet_rows, A)), shape((6, A, A), BF16),
+            shape((hid, R), BF16), shape((R, hid), BF16), shape((R, hid), BF16), shape((hid, R), BF16),
+        ),
+        in_specs=[SMEM_SPEC] * 2 + vmem(6),
+        out_specs=(vmem(1)[0], ANY_SPEC, *vmem(6)),
+        scratch_shapes=[
+            volume, volume, pltpu.VMEM((2, hid, cells), BF16), pltpu.VMEM((R, hid), F32),
+            pltpu.SemaphoreType.DMA((2, parts)),
+        ],
         compiler_params=params,
         name="first",
-    )(table, pick, pops, cot, w_in, w_mid, w_out)
+    )(face_level, face_quadrant, table, pops, cot, w_in.T, w_mid, w_out)
+    backs = (w_in_t, w_mid_t, w_out_t)
     recv = exchange(sheets, 0)
     post2, bar, sheets, grads = pl.pallas_call(
-        middle_kernel,
-        out_shape=(shape((R, cells)), shape((R, cells)), shape((3, 2 * R, A)), shape((total_rows, hid))),
+        functools.partial(middle_kernel, blocks),
+        out_shape=(shape((R, cells)), shape((R, cells)), shape((3, sheet_rows, A)), shape((total_rows, hid))),
         in_specs=[SMEM_SPEC] + vmem(11),
         out_specs=tuple(vmem(4)),
-        scratch_shapes=[volume] * 4,
+        scratch_shapes=[volume] * 4 + [tmp],
         compiler_params=params,
         name="middle",
-    )(slots, table, pick, recv, post1, cot, w_in, w_mid, w_out, *backs)
+    )(face_source, table, pick, recv, post1, cot, w_in, w_mid, w_out, *backs)
     recv = exchange(sheets, 1)
     final, grad_pops, grads = pl.pallas_call(
-        last_kernel,
-        out_shape=(shape((Q, cells)), shape((Q, cells)), shape((total_rows, hid))),
+        functools.partial(last_kernel, blocks),
+        out_shape=(shape(pops.shape), shape(pops.shape), shape((total_rows, hid))),
         in_specs=[SMEM_SPEC] + vmem(6) + [ANY_SPEC] + vmem(4),
         out_specs=tuple(vmem(3)),
-        scratch_shapes=[volume] * 3 + [pltpu.VMEM((2, hid, cells), BF16), pltpu.SemaphoreType.DMA((2, parts))],
+        scratch_shapes=[volume] * 3 + [tmp, pltpu.VMEM((2, hid, cells), BF16), pltpu.SemaphoreType.DMA((2, parts))],
         compiler_params=params,
         name="last",
-    )(slots, table, pick, recv, post2, bar, pops, hidden, grads, *backs)
-    rows, width = total_rows // blocks, hid // slabs
+    )(face_source, table, pick, recv, post2, bar, pops, hidden, grads, *backs)
+    chips = blocks // 2
+    rows, width = total_rows // (blocks * PIECES), hid // slabs
     total = pl.pallas_call(
-        functools.partial(sum_kernel, blocks, slabs),
+        functools.partial(sum_kernel, chips, slabs),
         out_shape=shape((total_rows, hid)),
         in_specs=vmem(1),
         out_specs=vmem(1)[0],
         scratch_shapes=[
-            pltpu.VMEM((blocks - 1, rows, hid), F32),
-            pltpu.VMEM((slabs - 1, rows, width), F32),
-            pltpu.VMEM((rows, hid), F32),
-            pltpu.SemaphoreType.DMA((2, blocks - 1)),
-            pltpu.SemaphoreType.DMA((2, slabs - 1)),
-            pltpu.SemaphoreType.DMA((2, blocks - 1)),
-            pltpu.SemaphoreType.DMA((2, slabs - 1)),
+            pltpu.VMEM((PIECES, chips * rows, hid), F32),
+            pltpu.VMEM((PIECES, chips * rows, hid), F32),
+            pltpu.VMEM((PIECES, chips - 1, rows, hid), F32),
+            pltpu.VMEM((PIECES, rows, hid), F32),
+            pltpu.VMEM((PIECES, slabs - 1, rows, width), F32),
+            pltpu.SemaphoreType.DMA((2, PIECES, 2 * (chips + slabs - 1))),
         ],
         compiler_params=pltpu.CompilerParams(collective_id=2, has_side_effects=True),
         name="sum_all",
     )(grads)
     total = total * float(blocks * slabs * cells) ** (-0.5)
     return (
-        final[:, None, None, :],
-        grad_pops[:, None, None, :],
+        final.reshape(populations.shape),
+        grad_pops.reshape(populations.shape),
         total[hid : hid + Q].T,
         total[:hid][None],
         total[hid + R : hid + R + Q],

time: 133 us -> 108 us (0.81)
  Pallas kernels: 113 us -> 101 us
  local copies, waits for them, and re-layouts: 13.3 us -> 5.07 us
  other arithmetic: 5.49 us -> 1.4 us
    pallas_call x3, Pallas kernels: 79.9 us -> 71.4 us  [the longest x1 32 us: shards(): pl.pallas_call(functools.partial(sum_kernel, chips, slabs), out_shape=sha...]
    unnamed x13 -> x2, local copies, waits for them, and re-layouts: 8.22 us -> 3.39 us
    pallas_call x2, Pallas kernels: 23.1 us -> 19.1 us  [exchange(): pl.pallas_call(functools.partial(exchange_kernel, blocks, slabs), out_sha...]
    transpose x2 -> x0, local copies, waits for them, and re-layouts: 2.06 us -> none  [shards(): backs = (w_in.T, w_mid.T, w_out.T)]
where the time goes in v2:
time: 108 us
  Pallas kernels  101 us (94%)
  local copies, waits for them, and re-layouts  5.07 us (5%)
  other arithmetic  1.4 us (1%)
    pallas_call x1, Pallas kernels, shards(): pl.pallas_call(functools.partial(sum_kernel, chips, slabs), out_shape=sha...  32 us
    pallas_call x1, Pallas kernels, shards(): pl.pallas_call(functools.partial(middle_kernel, blocks), out_shape=(shape...  22.1 us
    pallas_call x2, Pallas kernels, exchange(): pl.pallas_call(functools.partial(exchange_kernel, blocks, slabs), out_sha...  19.1 us
    pallas_call x1, Pallas kernels, shards(): pl.pallas_call(functools.partial(last_kernel, blocks), out_shape=(shape(p...  17.4 us
    pallas_call x1, Pallas kernels, shards(): pl.pallas_call(first_kernel, out_shape=(shape((R, cells)), shape((2, hid,...  10.4 us
    unnamed x2, local copies, waits for them, and re-layouts  3.39 us

profile of v2, /device:TPU:0, one launch (start us, length us, event | category | flops | bytes accessed | tf_op | source)
XLA Modules:
  0.0 108.1 jit_solution(9557591983122848425)
XLA Ops:
  0.6 1.3 %copy.25.source = s32[8,4]{1,0:T(8,128)} copy(s32[8,4]{0,1:T(4,128)} %param.14) | data formatting | bytes 256 | tf_op args[5]
  2.0 2.0 %copy.21 = bf16[1,512,512]{1,2,0:T(8,128)(2,1)} copy(bf16[1,512,512]{2,1,0:T(8,128)(2,1)} %param.11) | data formatting | bytes 1048576 | tf_op args[2]
  4.0 10.4 %first.1 = (f32[24,4096]{1,0:T(8,128)}, bf16[2,512,4096]{2,1,0:T(8,128)(2,1)}, f32[3,24,256]{2,1,0:T(8,128)}, bf16[6,256,256]{2,1,0:T(8,128)(2,1)}, bf16[512,24]...) custom-call(s32[1,1,6]{2,1,0:T(1,128)} %level.1, ...), custom_call_target="tpu_custom_call" | custom-call | tf_op jit(solution)/shard_map/first/pallas_call | solution.py:561
  14.5 11.4 %exchange0.1.recv = f32[9,24,256]{2,1,0:T(8,128)} custom-call(f32[3,24,256]{2,1,0:T(8,128)} %get-tuple-element.21.sheets), custom_call_target="tpu_custom_call" | custom-call | tf_op jit(solution)/shard_map/exchange0/pallas_call | solution.py:551
  25.8 22.1 %middle.1 = (f32[24,4096]{1,0:T(8,128)}, f32[24,4096]{1,0:T(8,128)}, f32[3,24,256]{2,1,0:T(8,128)}, f32[576,512]{1,0:T(8,128)}) custom-call(s32[8,4]{1,0:T(8,128)} %copy.25.source, s32[4,24,256]{2,1,0:T(8,128)} %constant.4.clone.table, bf16[6,256,256]{2,1,0:T(8,128)(2,1)} %get-tuple-element.20.pick, f32[9,24,256]{2,1,0:T(8,128)} %exchange0.1.recv, ...), custom_call_target="tpu_custom_call" | custom-call | tf_op jit(solution)/shard_map/middle/pallas_call | solution.py:578
  47.9 7.7 %exchange1.1.recv = f32[9,24,256]{2,1,0:T(8,128)} custom-call(f32[3,24,256]{2,1,0:T(8,128)} %get-tuple-element.27.sheets), custom_call_target="tpu_custom_call" | custom-call | tf_op jit(solution)/shard_map/exchange1/pallas_call | solution.py:551
  55.7 17.4 %last.1 = (f32[608,128]{1,0:T(8,128)}, f32[608,128]{1,0:T(8,128)}, f32[576,512]{1,0:T(8,128)}) custom-call(s32[8,4]{1,0:T(8,128)} %copy.25.source, s32[4,24,256]{2,1,0:T(8,128)} %constant.4.clone.table, bf16[6,256,256]{2,1,0:T(8,128)(2,1)} %get-tuple-element.20.pick, f32[9,24,256]{2,1,0:T(8,128)} %exchange1.1.recv, f32[24,4096]{1,0:T(8,128)} %get-tuple-element.28.post2, ...), custom_call_target="tpu_custom_call" | custom-call | tf_op jit(solution)/shard_map/last/pallas_call | solution.py:588
  73.0 32.0 %sum_all.1 = f32[576,512]{1,0:T(8,128)} custom-call(f32[576,512]{1,0:T(8,128)} %get-tuple-element.34.grads), custom_call_target="tpu_custom_call" | custom-call | tf_op jit(solution)/shard_map/sum_all/pallas_call | solution.py:599
  105.0 1.4 %broadcast_multiply_fusion = f32[576,512]{1,0:T(8,128)S(1)} fusion(f32[576,512]{1,0:T(8,128)} %sum_all.1), kind=kLoop, calls=%fused_computation.1 | loop fusion | flops 294912 | bytes 2359296 | tf_op jit(solution)/shard_map/mul | solution.py:615
  106.4 0.6 fusion
  107.0 1.0 slice_bitcast_fusion

commit v3 on v2

--- a/solution.py
+++ b/solution.py
@@ -12,7 +12,7 @@
 R = 24
 S = 16
 A = S * S
-CHUNK = 512
+CHUNK = 1024
 MESH = pl.DeviceIdType.MESH
 F32, BF16 = jnp.float32, jnp.bfloat16
 
@@ -146,7 +146,7 @@
 
 def slot_of(source_ref, blocks, face):
     me = lax.axis_index("blocks")
-    distance = lax.rem(source_ref[me, face] - me + blocks, blocks)
+    distance = lax.rem(source_ref[face, me] - me + blocks, blocks)
     distance = jnp.where(distance > blocks // 2, distance - blocks, distance)
     slot = jnp.where(distance < 0, distance + REACH, distance + REACH - 1)
     return jnp.clip(slot, 0, 2 * REACH - 1)
@@ -315,7 +315,7 @@
 
 def first_kernel(
     level, quadrant, table, pops, cot, w_in_rows, w_mid, w_out_rows,
-    post, h_hbm, sheets, pick, w_in, w_in_t, w_out, w_out_t, wide, cot_wide, h_buf, tall, sems,
+    post, h_hbm, sheets, pick, w_in, w_in_t, w_out, w_out_t, w_mid_t, wide, cot_wide, h_buf, tall, sems,
 ):
     g = Geometry(table)
     cells = wide.shape[1]
@@ -323,6 +323,7 @@
     load_rows(cot_wide, cot)
     padded_rows(w_in_rows, tall, w_in_t, w_in)
     padded_rows(w_out_rows, tall, w_out, w_out_t)
+    w_mid_t[...] = w_mid[...].astype(F32).T.astype(BF16)
     one_hot_layers(level, quadrant, pick)
     sheets[...] = jnp.zeros(sheets.shape, F32)
 
@@ -512,10 +513,14 @@
             spot = out.at[half_of(p, core)]
             flying[p] = [send(spot, spot, p, again, twin)]
 
-    for tick in range(6 + PIECES):
+    for number in (0, 1):
         for p in range(PIECES):
-            if 0 <= tick - p <= 6:
-                stage(p, tick - p)
+            stage(p, number)
+    for tick in range(2, 5 + PIECES + 2):
+        for p in range(PIECES):
+            number = tick - p
+            if 2 <= number <= 6:
+                stage(p, number)
 
 
 def vmem(count):
@@ -537,7 +542,6 @@
     pops, cot = (v.reshape(Q * cells // LANES, LANES) for v in (populations, cotangent))
     table = jnp.asarray(row_table())
     w_mid = w_mid[0]
-    w_mid_t = w_mid.T
     step = 8 * blocks * PIECES
     total_rows = -(-(hid + 2 * R) // step) * step
     parts = cells // CHUNK
@@ -558,14 +562,15 @@
             name=f"exchange{which}",
         )(sheets)
 
-    post1, hidden, sheets, pick, w_in, w_in_t, w_out, w_out_t = pl.pallas_call(
+    post1, hidden, sheets, pick, w_in, w_in_t, w_out, w_out_t, w_mid_t = pl.pallas_call(
         first_kernel,
         out_shape=(
             shape((R, cells)), shape((2, hid, cells), BF16), shape((3, sheet_rows, A)), shape((6, A, A), BF16),
             shape((hid, R), BF16), shape((R, hid), BF16), shape((R, hid), BF16), shape((hid, R), BF16),
+            shape((hid, hid), BF16),
         ),
         in_specs=[SMEM_SPEC] * 2 + vmem(6),
-        out_specs=(vmem(1)[0], ANY_SPEC, *vmem(6)),
+        out_specs=(vmem(1)[0], ANY_SPEC, *vmem(7)),
         scratch_shapes=[
             volume, volume, pltpu.VMEM((2, hid, cells), BF16), pltpu.VMEM((R, hid), F32),
             pltpu.SemaphoreType.DMA((2, parts)),
@@ -583,7 +588,7 @@
         scratch_shapes=[volume] * 4 + [tmp],
         compiler_params=params,
         name="middle",
-    )(face_source, table, pick, recv, post1, cot, w_in, w_mid, w_out, *backs)
+    )(face_source.T, table, pick, recv, post1, cot, w_in, w_mid, w_out, *backs)
     recv = exchange(sheets, 1)
     final, grad_pops, grads = pl.pallas_call(
         functools.partial(last_kernel, blocks),
@@ -593,7 +598,7 @@
         scratch_shapes=[volume] * 3 + [tmp, pltpu.VMEM((2, hid, cells), BF16), pltpu.SemaphoreType.DMA((2, parts))],
         compiler_params=params,
         name="last",
-    )(face_source, table, pick, recv, post2, bar, pops, hidden, grads, *backs)
+    )(face_source.T, table, pick, recv, post2, bar, pops, hidden, grads, *backs)
     chips = blocks // 2
     rows, width = total_rows // (blocks * PIECES), hid // slabs
     total = pl.pallas_call(

time: 108 us -> 102 us (0.944)
  Pallas kernels: 101 us -> 97.6 us
  local copies, waits for them, and re-layouts: 5.07 us -> 1.68 us
    unnamed x2 -> x0, local copies, waits for them, and re-layouts: 3.39 us -> none
    pallas_call x1, Pallas kernels: 22.1 us -> 20 us  [shards(): pl.pallas_call(functools.partial(middle_kernel, blocks), out_shape=(shape...]
    pallas_call x1, Pallas kernels: 10.4 us -> 9.32 us  [shards(): pl.pallas_call(first_kernel, out_shape=(shape((R, cells)), shape((2, hid,...]
where the time goes in v3:
time: 102 us; the launch traced here: 101 us
  Pallas kernels  97.6 us (96%)
  local copies, waits for them, and re-layouts  1.68 us (2%)
  other arithmetic  1.4 us (1%)
    pallas_call x1, Pallas kernels, shards(): pl.pallas_call(functools.partial(sum_kernel, chips, slabs), out_shape=sha...  32.5 us
    pallas_call x1, Pallas kernels, shards(): pl.pallas_call(functools.partial(middle_kernel, blocks), out_shape=(shape...  20 us
    pallas_call x2, Pallas kernels, exchange(): pl.pallas_call(functools.partial(exchange_kernel, blocks, slabs), out_sha...  19.1 us
    pallas_call x1, Pallas kernels, shards(): pl.pallas_call(functools.partial(last_kernel, blocks), out_shape=(shape(p...  16.7 us
    pallas_call x1, Pallas kernels, shards(): pl.pallas_call(first_kernel, out_shape=(shape((R, cells)), shape((2, hid,...  9.32 us

profile of v3, /device:TPU:0, one launch (start us, length us, event | category | flops | bytes accessed | tf_op | source)
XLA Modules:
  0.0 101.4 jit_solution(1546371014430421422)
XLA Ops:
  0.6 9.3 %first.1 = (f32[24,4096]{1,0:T(8,128)}, bf16[2,512,4096]{2,1,0:T(8,128)(2,1)}, f32[3,24,256]{2,1,0:T(8,128)}, bf16[6,256,256]{2,1,0:T(8,128)(2,1)}, bf16[512,24]...) custom-call(s32[1,1,6]{2,1,0:T(1,128)} %level.1, ...), custom_call_target="tpu_custom_call" | custom-call | tf_op jit(solution)/shard_map/first/pallas_call | solution.py:565
  10.0 11.4 %exchange0.1.recv = f32[9,24,256]{2,1,0:T(8,128)} custom-call(f32[3,24,256]{2,1,0:T(8,128)} %get-tuple-element.22.sheets), custom_call_target="tpu_custom_call" | custom-call | tf_op jit(solution)/shard_map/exchange0/pallas_call | solution.py:555
  21.3 20.0 %middle.1 = (f32[24,4096]{1,0:T(8,128)}, f32[24,4096]{1,0:T(8,128)}, f32[3,24,256]{2,1,0:T(8,128)}, f32[576,512]{1,0:T(8,128)}) custom-call(s32[4,8]{1,0:T(4,128)} %bitcast.18, s32[4,24,256]{2,1,0:T(8,128)} %constant.4.clone.table, bf16[6,256,256]{2,1,0:T(8,128)(2,1)} %get-tuple-element.21.pick, f32[9,24,256]{2,1,0:T(8,128)} %exchange0.1.recv, ...), custom_call_target="tpu_custom_call" | custom-call | tf_op jit(solution)/shard_map/middle/pallas_call | solution.py:583
  41.4 7.7 %exchange1.1.recv = f32[9,24,256]{2,1,0:T(8,128)} custom-call(f32[3,24,256]{2,1,0:T(8,128)} %get-tuple-element.29.sheets), custom_call_target="tpu_custom_call" | custom-call | tf_op jit(solution)/shard_map/exchange1/pallas_call | solution.py:555
  49.1 16.7 %last.1 = (f32[608,128]{1,0:T(8,128)}, f32[608,128]{1,0:T(8,128)}, f32[576,512]{1,0:T(8,128)}) custom-call(s32[4,8]{1,0:T(4,128)} %bitcast.19, s32[4,24,256]{2,1,0:T(8,128)} %constant.4.clone.table, bf16[6,256,256]{2,1,0:T(8,128)(2,1)} %get-tuple-element.21.pick, f32[9,24,256]{2,1,0:T(8,128)} %exchange1.1.recv, f32[24,4096]{1,0:T(8,128)} %get-tuple-element.30.post2, ...), custom_call_target="tpu_custom_call" | custom-call | tf_op jit(solution)/shard_map/last/pallas_call | solution.py:593
  65.8 32.5 %sum_all.1 = f32[576,512]{1,0:T(8,128)} custom-call(f32[576,512]{1,0:T(8,128)} %get-tuple-element.36.grads), custom_call_target="tpu_custom_call" | custom-call | tf_op jit(solution)/shard_map/sum_all/pallas_call | solution.py:604
  98.3 1.4 %broadcast_multiply_fusion = f32[576,512]{1,0:T(8,128)S(1)} fusion(f32[576,512]{1,0:T(8,128)} %sum_all.1), kind=kLoop, calls=%fused_computation.1 | loop fusion | flops 294912 | bytes 2359296 | tf_op jit(solution)/shard_map/mul | solution.py:620
  99.7 0.6 fusion
  100.3 1.0 %slice_bitcast_fusion = f32[1,512,512]{2,1,0:T(8,128)} fusion(f32[576,512]{1,0:T(8,128)S(1)} %broadcast_multiply_fusion), kind=kLoop, calls=%fused_computation | loop fusion | bytes 2097152 | tf_op jit(solution)/shard_map/broadcast_in_dim | solution.py:625

commit v4 on v3

--- a/solution.py
+++ b/solution.py
@@ -478,10 +478,13 @@
     first_t, first_s = 1, len(sides) + 1
     again = len(sides) + len(stack) + 1
     flying = [[] for _ in range(PIECES)]
+    sent = []
 
     def stage(p, number):
         for copy in flying[p]:
-            copy.wait()
+            copy.wait_recv()
+        sent.extend(flying[p])
+        flying[p] = []
         if number == 0:
             flying[p] = [send(grads.at[half_of(p, 1 - core)], land_c.at[p], p, 0, twin)]
         if number == 1:
@@ -521,6 +524,8 @@
             number = tick - p
             if 2 <= number <= 6:
                 stage(p, number)
+    for copy in sent:
+        copy.wait_send()
 
 
 def vmem(count):

time: 102 us -> 100 us (0.980)
  Pallas kernels: 97.6 us -> 96.2 us
    pallas_call x1, Pallas kernels: 32.5 us -> 31.1 us  [shards(): pl.pallas_call(functools.partial(sum_kernel, chips, slabs), out_shape=sha...]
where the time goes in v4:
time: 100 us
  Pallas kernels  96.2 us (96%)
  local copies, waits for them, and re-layouts  1.68 us (2%)
  other arithmetic  1.4 us (1%)
    pallas_call x1, Pallas kernels, shards(): pl.pallas_call(functools.partial(sum_kernel, chips, slabs), out_shape=sha...  31.1 us
    pallas_call x1, Pallas kernels, shards(): pl.pallas_call(functools.partial(middle_kernel, blocks), out_shape=(shape...  20 us
    pallas_call x2, Pallas kernels, exchange(): pl.pallas_call(functools.partial(exchange_kernel, blocks, slabs), out_sha...  19.1 us
    pallas_call x1, Pallas kernels, shards(): pl.pallas_call(functools.partial(last_kernel, blocks), out_shape=(shape(p...  16.7 us
    pallas_call x1, Pallas kernels, shards(): pl.pallas_call(first_kernel, out_shape=(shape((R, cells)), shape((2, hid,...  9.32 us

profile of v4, /device:TPU:0, one launch (start us, length us, event | category | flops | bytes accessed | tf_op | source)
XLA Modules:
  0.0 100.0 jit_solution(16810472117545681957)
XLA Ops:
  0.6 9.3 %first.1 = (f32[24,4096]{1,0:T(8,128)}, bf16[2,512,4096]{2,1,0:T(8,128)(2,1)}, f32[3,24,256]{2,1,0:T(8,128)}, bf16[6,256,256]{2,1,0:T(8,128)(2,1)}, bf16[512,24]...) custom-call(s32[1,1,6]{2,1,0:T(1,128)} %level.1, ...), custom_call_target="tpu_custom_call" | custom-call | tf_op jit(solution)/shard_map/first/pallas_call | solution.py:570
  10.0 11.4 %exchange0.1.recv = f32[9,24,256]{2,1,0:T(8,128)} custom-call(f32[3,24,256]{2,1,0:T(8,128)} %get-tuple-element.22.sheets), custom_call_target="tpu_custom_call" | custom-call | tf_op jit(solution)/shard_map/exchange0/pallas_call | solution.py:560
  21.3 20.0 %middle.1 = (f32[24,4096]{1,0:T(8,128)}, f32[24,4096]{1,0:T(8,128)}, f32[3,24,256]{2,1,0:T(8,128)}, f32[576,512]{1,0:T(8,128)}) custom-call(s32[4,8]{1,0:T(4,128)} %bitcast.18, s32[4,24,256]{2,1,0:T(8,128)} %constant.4.clone.table, bf16[6,256,256]{2,1,0:T(8,128)(2,1)} %get-tuple-element.21.pick, f32[9,24,256]{2,1,0:T(8,128)} %exchange0.1.recv, ...), custom_call_target="tpu_custom_call" | custom-call | tf_op jit(solution)/shard_map/middle/pallas_call | solution.py:588
  41.4 7.7 %exchange1.1.recv = f32[9,24,256]{2,1,0:T(8,128)} custom-call(f32[3,24,256]{2,1,0:T(8,128)} %get-tuple-element.29.sheets), custom_call_target="tpu_custom_call" | custom-call | tf_op jit(solution)/shard_map/exchange1/pallas_call | solution.py:560
  49.1 16.7 %last.1 = (f32[608,128]{1,0:T(8,128)}, f32[608,128]{1,0:T(8,128)}, f32[576,512]{1,0:T(8,128)}) custom-call(s32[4,8]{1,0:T(4,128)} %bitcast.19, s32[4,24,256]{2,1,0:T(8,128)} %constant.4.clone.table, bf16[6,256,256]{2,1,0:T(8,128)(2,1)} %get-tuple-element.21.pick, f32[9,24,256]{2,1,0:T(8,128)} %exchange1.1.recv, f32[24,4096]{1,0:T(8,128)} %get-tuple-element.30.post2, ...), custom_call_target="tpu_custom_call" | custom-call | tf_op jit(solution)/shard_map/last/pallas_call | solution.py:598
  65.8 31.1 %sum_all.1 = f32[576,512]{1,0:T(8,128)} custom-call(f32[576,512]{1,0:T(8,128)} %get-tuple-element.36.grads), custom_call_target="tpu_custom_call" | custom-call | tf_op jit(solution)/shard_map/sum_all/pallas_call | solution.py:609
  96.9 1.4 %broadcast_multiply_fusion = f32[576,512]{1,0:T(8,128)S(1)} fusion(f32[576,512]{1,0:T(8,128)} %sum_all.1), kind=kLoop, calls=%fused_computation.1 | loop fusion | flops 294912 | bytes 2359296 | tf_op jit(solution)/shard_map/mul | solution.py:625
  98.3 0.6 fusion
  98.9 1.0 %slice_bitcast_fusion = f32[1,512,512]{2,1,0:T(8,128)} fusion(f32[576,512]{1,0:T(8,128)S(1)} %broadcast_multiply_fusion), kind=kLoop, calls=%fused_computation | loop fusion | bytes 2097152 | tf_op jit(solution)/shard_map/broadcast_in_dim | solution.py:630
